TPU v7x, 256 devices: a whole 4x4x8 slice. The times are simulated.
256 devices in a mesh: seq: 64 (over z, y, core), grp: 4 (over x).
Axes of the slice: x: 4, y: 4, z: 8, core: 2. Of those that a mesh axis runs over, the one named last changes fastest.
Arguments:
- q_nope: bfloat16 [1024, 128, 128], P('seq', 'grp'), may hold values from -6 to 6
- q_rope: bfloat16 [1024, 128, 64], P('seq', 'grp'), may hold values from -256 to 256
- cache: bfloat16 [65536, 576], P('seq'), may hold values from -6 to 6
- w_uk: bfloat16 [128, 65536], P('grp', 'seq'), may hold values from -0.5 to 0.5
- w_uv: bfloat16 [128, 65536], P('grp', 'seq'), may hold values from -0.25 to 0.25
- d_out: bfloat16 [1024, 128, 128], P('seq', 'grp'), may hold values from -6 to 6
- sel: int32 [1024, 32], P('seq'), may hold values from 0 to 63, as said below
- slot_blocks: int32 [64, 64], P('seq'), may hold values from 0 to 15, as said below
Outputs:
- attn_out: bfloat16 [1024, 128, 128], P('seq', 'grp')
- d_q_nope: bfloat16 [1024, 128, 128], P('seq', 'grp')
- d_q_rope: bfloat16 [1024, 128, 64], P('seq', 'grp')
- d_cache: float32 [65536, 576], P('seq')
Inputs may be any that keep to these rules, and one draw needn't show every extreme that they name: `sel`: each row names 32 different places; place s stands for the block that the row's device asks of device s. `slot_blocks`: entry [r, s] is the index among device s's own blocks of the block that device r asks for in place s; the 1 entries of a row toward one device differ.
All inputs are finite; a program needn't handle non-finite values.
Results may differ from a plain program's by a relative error of at most 0.015.
Values may be sent and summed in bfloat16 or wider, within the bound.
A program may use at most 128 MiB of HBM per device.

v0:
```python
import math

import jax
import jax.numpy as jnp
from jax import lax
from jax.sharding import PartitionSpec as P

BLOCK_LEN = 64


def local(q_nope, q_rope, cache, w_uk, w_uv, d_out, sel, slot_blocks):
    peers = lax.axis_size("seq")
    queries, heads, nope = q_nope.shape
    rope = q_rope.shape[2]
    width = cache.shape[1]
    latent = width - rope
    value = d_out.shape[2]
    slot_total = slot_blocks.shape[1]
    per_peer = slot_total // peers
    own_blocks = cache.shape[0] // BLOCK_LEN
    scale = 1.0 / math.sqrt(nope + rope)
    gathered_k, gathered_v = (
        lax.all_gather(w_uk, "seq", axis=1, tiled=True),
        lax.all_gather(w_uv, "seq", axis=1, tiled=True),
    )
    weight_k = gathered_k.reshape(heads, nope, latent)
    weight_v = gathered_v.reshape(heads, latent, value)
    wanted = slot_blocks.reshape(peers, per_peer)
    asked = lax.all_to_all(wanted, "seq", split_axis=0, concat_axis=0, tiled=True)
    blocks = cache.reshape(own_blocks, BLOCK_LEN, width)
    arrived = lax.all_to_all(blocks[asked], "seq", split_axis=0, concat_axis=0, tiled=True)
    keys = arrived.reshape(slot_total * BLOCK_LEN, width)
    keys_lat = keys[:, :latent]
    q_lat = jnp.einsum("qhn,hnl->qhl", q_nope, weight_k, preferred_element_type=jnp.float32).astype(
        jnp.bfloat16
    )
    qfull = jnp.concatenate([q_lat, q_rope], axis=-1)
    chosen = jnp.any(
        sel[:, :, None] == jnp.arange(slot_total, dtype=jnp.int32)[None, None, :], axis=1
    )
    live = jnp.repeat(chosen, BLOCK_LEN, axis=1)[:, None, :]
    score = jnp.einsum("qhc,tc->qht", qfull, keys, preferred_element_type=jnp.float32) * scale
    score = jnp.where(live, score, -jnp.inf)
    prob = jax.nn.softmax(score, axis=-1)
    prob_low = prob.astype(jnp.bfloat16)
    olat = jnp.einsum("qht,tl->qhl", prob_low, keys_lat, preferred_element_type=jnp.float32).astype(
        jnp.bfloat16
    )
    attn_out = jnp.einsum(
        "qhl,hlv->qhv", olat, weight_v, preferred_element_type=jnp.float32
    ).astype(jnp.bfloat16)
    d_olat = jnp.einsum("qhv,hlv->qhl", d_out, weight_v, preferred_element_type=jnp.float32).astype(
        jnp.bfloat16
    )
    dprob = jnp.einsum("qhl,tl->qht", d_olat, keys_lat, preferred_element_type=jnp.float32)
    delta = jnp.sum(prob * dprob, axis=-1, keepdims=True)
    dscore = (prob * (dprob - delta) * scale).astype(jnp.bfloat16)
    dquery = jnp.einsum("qht,tc->qhc", dscore, keys, preferred_element_type=jnp.float32)
    d_q_rope = dquery[:, :, latent:].astype(jnp.bfloat16)
    d_qlat = dquery[:, :, :latent].astype(jnp.bfloat16)
    d_q_nope = jnp.einsum(
        "qhl,hnl->qhn", d_qlat, weight_k, preferred_element_type=jnp.float32
    ).astype(jnp.bfloat16)
    value_part = jnp.einsum("qht,qhl->tl", prob_low, d_olat, preferred_element_type=jnp.float32)
    dkeys = jnp.einsum("qht,qhc->tc", dscore, qfull, preferred_element_type=jnp.float32)
    dkeys = dkeys + jnp.pad(value_part, ((0, 0), (0, rope)))
    one_hot = (
        asked.reshape(-1)[:, None] == jnp.arange(own_blocks, dtype=jnp.int32)[None, :]
    ).astype(jnp.float32)
    returned = lax.all_to_all(
        dkeys.reshape(peers, per_peer, BLOCK_LEN * width).astype(jnp.bfloat16),
        "seq",
        split_axis=0,
        concat_axis=0,
        tiled=True,
    ).astype(jnp.float32)
    local_grad = jnp.dot(
        one_hot.T,
        returned.reshape(peers * per_peer, BLOCK_LEN * width),
        precision=lax.Precision.HIGHEST,
    )
    d_cache = (
        lax.psum(local_grad.astype(jnp.bfloat16), "grp")
        .astype(jnp.float32)
        .reshape(own_blocks * BLOCK_LEN, width)
    )
    return (attn_out, d_q_nope, d_q_rope, d_cache)


def solution(mesh):
    return jax.shard_map(
        local,
        mesh=mesh,
        in_specs=(
            P("seq", "grp", None),
            P("seq", "grp", None),
            P("seq", None),
            P("grp", "seq"),
            P("grp", "seq"),
            P("seq", "grp", None),
            P("seq", None),
            P("seq", None),
        ),
        out_specs=(
            P("seq", "grp", None),
            P("seq", "grp", None),
            P("seq", "grp", None),
            P("seq", None),
        ),
        check_vma=False,
    )
```

profile of v0, /device:TPU:1, one launch (start us, length us, event | category | flops | bytes accessed | tf_op | source)
XLA Modules:
  0.0 523.4 jit_solution(6179962597997448510)
XLA Ops:
  7.2 0.0 copy-start
  7.2 0.0 all-gather.5.cloned.1.call-start
  7.2 0.7 all-gather.5.cloned.1.call-update
  7.9 1.4 copy.80
  9.3 13.1 %all-to-all-start = ((s32[64,1,1]{2,1,0:T(1,128)}), s32[64,1,1]{2,1,0:T(1,128)S(1)}, u32[]{:S(2)}, u32[]{:S(2)}) async-start(s32[64,1,1]{2,1,0:T(1,128)} %copy.80), calls=%async_computation | async-start | bytes 65536 | tf_op jit(solution)/shard_map/all_to_all | solution.py:29
  22.4 1.7 copy.79
  24.1 7.6 %all-to-all-done = s32[64,1,1]{2,1,0:T(1,128)S(1)} async-done(((s32[64,1,1]{2,1,0:T(1,128)}), s32[64,1,1]{2,1,0:T(1,128)S(1)}, u32[]{:S(2)}, u32[]{:S(2)}) %all-to-all-start) | async-done | bytes 288 | tf_op jit(solution)/shard_map/all_to_all | solution.py:29
  31.8 2.4 fusion.49
  34.1 3.5 gather_fusion
  37.6 0.0 copy-start.7
  37.6 0.0 copy-start.6
  37.6 5.9 %all-to-all-start.1 = ((bf16[64,1,64,576]{3,2,1,0:T(8,128)(2,1)}), bf16[64,1,64,576]{3,2,1,0:T(8,128)(2,1)}, u32[]{:S(2)}, u32[]{:S(2)}) async-start(bf16[64,1,64,576]{3,2,1,0:T(8,128)(2,1)} %bitcast.47), calls=%async_computation.1 | async-start | bytes 10485760 | tf_op jit(solution)/shard_map/all_to_all | solution.py:31
  43.5 0.5 all-gather.3.cloned.1.call-start
  44.0 0.2 all-gather.3.cloned.1.call-update
  44.2 0.0 copy-done.7
  44.3 0.2 fusion.38
  44.4 0.2 broadcast_in_dim.24
  44.6 0.2 broadcast_in_dim.25
  44.9 0.0 copy-done.6
  44.9 0.1 copy.78
  44.9 66.9 %all-gather.5.cloned.1.call-done = bf16[32,65536]{1,0:T(8,128)(2,1)} async-done(((bf16[32,1024]{1,0:T(8,128)(2,1)}), bf16[32,65536]{1,0:T(8,128)(2,1)}) %all-gather.5.cloned.1.call-update) | async-done | bytes 4194320 | tf_op jit(solution)/shard_map/all_gather | solution.py:24
  111.9 5.1 copy.102
  117.0 0.0 copy-start.5
  117.0 80.6 %all-gather.3.cloned.1.call-done = bf16[32,65536]{1,0:T(8,128)(2,1)} async-done(((bf16[32,1024]{1,0:T(8,128)(2,1)}), bf16[32,65536]{1,0:T(8,128)(2,1)}) %all-gather.3.cloned.1.call-update) | async-done | bytes 4194320 | tf_op jit(solution)/shard_map/all_gather | solution.py:23
  197.6 0.0 copy-start.2
  197.6 3.9 copy.101
  201.5 0.0 copy-start.3
  201.5 2.1 copy-done.3
  203.5 0.0 copy-done.5
  203.5 0.6 fusion.28
  204.2 0.1 pad_maximum_fusion
  204.3 0.0 copy-done
  204.3 0.0 copy-done.2
  204.3 1.2 fusion.27
  205.5 0.0 all-to-all-done.1
  205.5 8.0 %fusion.12 = f32[16,32,4096]{2,1,0:T(8,128)} fusion(bf16[4096,576]{1,0:T(8,128)(2,1)} %bitcast.5, bf16[16,32,512]{2,0,1:T(8,128)(2,1)S(1)} %fusion.27), kind=kOutput, calls=%fused_computation.20 | convolution fusion | flops 2147483648 | bytes 13107200 | tf_op jit(solution)/shard_map/qhl,tl->qht/dot_general | solution.py:55
  213.4 10.7 %fusion.50 = (f32[16,32]{1,0:T(8,128)S(1)}, f32[16,32,4096]{2,1,0:T(8,128)}) fusion(pred[16,4096]{1,0:T(8,128)(4,1)S(1)} %broadcast_in_dim.25, bf16[4096,576,1]{1,0,2:T(8,128)(2,1)} %bitcast.6, bf16[16,32,576]{2,0,1:T(8,128)(2,1)S(1)} %pad_maximum_fusion), kind=kOutput, calls=%fused_computation.59 | convolution fusion | flops 2424311808 | bytes 13764608 | tf_op jit(solution)/shard_map/sub | solution.py:44
  224.1 9.4 %convolution_bitcast_fusion = f32[4096,512]{0,1:T(8,128)} fusion(bf16[16,32,512]{2,0,1:T(8,128)(2,1)S(1)} %fusion.27, f32[16,32,4096]{2,1,0:T(8,128)} %get-tuple-element.27, f32[16,32]{1,0:T(8,128)S(1)} %get-tuple-element.26), kind=kOutput, calls=%fused_computation.12 | convolution fusion | flops 2151677952 | bytes 17303552 | tf_op jit(solution)/shard_map/qht,qhl->tl/dot_general | solution.py:64
  233.5 18.8 %fusion.2 = bf16[4096,576]{0,1:T(8,128)(2,1)} fusion(f32[4096,512]{0,1:T(8,128)} %convolution_bitcast_fusion, f32[16,32,4096]{2,1,0:T(8,128)} %fusion.12, bf16[16,32,576]{2,0,1:T(8,128)(2,1)S(1)} %pad_maximum_fusion, f32[16,32,4096]{2,1,0:T(8,128)} %get-tuple-element.27, f32[16,32]{1,0:T(8,128)S(1)} %get-tuple-element.26), kind=kOutput, calls=%fused_computation.5 | convolution fusion | flops 2435322368 | bytes 30476288 | tf_op jit(solution)/shard_map/qht,qhc->tc/dot_general | solution.py:65
  252.3 7.6 %copy.91 = bf16[4096,576]{1,0:T(8,128)(2,1)} copy(bf16[4096,576]{0,1:T(8,128)(2,1)} %fusion.2) | data formatting | bytes 9437184 | tf_op jit(solution)/shard_map/convert_element_type | solution.py:71
  259.9 21.7 %convert_element_type.71 = bf16[64,1,36864]{2,1,0:T(2,128)(2,1)} reshape(bf16[4096,576]{1,0:T(8,128)(2,1)} %copy.91) | data formatting | bytes 9437184 | tf_op jit(solution)/shard_map/convert_element_type | solution.py:71
  281.7 0.5 broadcast.36
  282.2 29.9 %reduce.4 = bf16[64,36864]{1,0:T(8,128)(2,1)} reduce(bf16[64,1,36864]{2,1,0:T(2,128)(2,1)} %convert_element_type.71, bf16[]{:T(256)} %broadcast.36), dimensions={1}, to_apply=%convert_element_type.71.reduce_sub_computation | reduce | bytes 9437186 | tf_op jit(solution)/shard_map/convert_element_type | solution.py:71
  312.1 8.3 %reshape.84 = bf16[64,2,18432]{2,1,0:T(2,128)(2,1)} reshape(bf16[64,36864]{1,0:T(8,128)(2,1)} %reduce.4) | data formatting | bytes 9437184
  320.4 6.6 %all-to-all-start.2 = ((bf16[64,2,18432]{2,1,0:T(2,128)(2,1)}), bf16[64,2,18432]{2,1,0:T(2,128)(2,1)}, u32[]{:S(2)}, u32[]{:S(2)}) async-start(bf16[64,2,18432]{2,1,0:T(2,128)(2,1)} %reshape.84), calls=%async_computation.2 | async-start | bytes 9437184 | tf_op jit(solution)/shard_map/all_to_all | solution.py:70
  326.9 0.3 all-reduce.3.cloned.1.call-start
  327.2 7.0 %fusion.24 = bf16[16,32,512]{2,1,0:T(8,128)(2,1)S(1)} fusion(bf16[4096,576]{1,0:T(8,128)(2,1)} %bitcast.5, f32[16,32,4096]{2,1,0:T(8,128)} %get-tuple-element.27, f32[16,32]{1,0:T(8,128)S(1)} %get-tuple-element.26), kind=kOutput, calls=%fused_computation.26 | convolution fusion | flops 2151940096 | bytes 13109248 | tf_op jit(solution)/shard_map/qht,tl->qhl/dot_general | solution.py:46
  334.2 98.3 %all-to-all-done.2 = bf16[64,2,18432]{2,1,0:T(2,128)(2,1)} async-done(((bf16[64,2,18432]{2,1,0:T(2,128)(2,1)}), bf16[64,2,18432]{2,1,0:T(2,128)(2,1)}, u32[]{:S(2)}, u32[]{:S(2)}) %all-to-all-start.2) | async-done | bytes 4718624 | tf_op jit(solution)/shard_map/all_to_all | solution.py:70
  432.6 20.2 %reshape.85 = bf16[64,1,36864]{2,1,0:T(2,128)(2,1)} reshape(bf16[64,2,18432]{2,1,0:T(2,128)(2,1)} %all-to-all-done.2) | data formatting | bytes 9437184
  452.7 8.8 %convolution_convert_fusion = bf16[16,36864]{1,0:T(8,128)(2,1)S(1)} fusion(bf16[64,1,36864]{2,1,0:T(2,128)(2,1)} %reshape.85, s32[64]{0:T(128)S(1)} %get-tuple-element.24), kind=kOutput, calls=%fused_computation.3 | convolution fusion | flops 76088320 | bytes 5898496 | tf_op jit(solution)/shard_map/dot_general | solution.py:77
  461.5 2.5 reshape.67
  464.0 0.0 all-reduce.3.cloned.1.call-update
  464.0 14.8 %fusion.21 = bf16[16,32,576]{2,1,0:T(8,128)(2,1)S(1)} fusion(bf16[4096,576,1]{1,0,2:T(8,128)(2,1)} %bitcast.6, f32[16,32,4096]{2,1,0:T(8,128)} %fusion.12, f32[16,32,4096]{2,1,0:T(8,128)} %get-tuple-element.27, f32[16,32]{1,0:T(8,128)S(1)} %get-tuple-element.26), kind=kOutput, calls=%fused_computation.25 | convolution fusion | flops 2430898688 | bytes 22087680 | tf_op jit(solution)/shard_map/qht,tc->qhc/dot_general | solution.py:58
  478.8 0.0 copy-start.4
  478.8 0.7 slice.18
  479.5 0.0 copy-start.1
  479.5 3.5 fusion.29
  483.1 0.7 copy.93
  483.8 0.0 copy-done.4
  483.8 1.2 fusion.30
  485.0 0.7 copy.94
  485.7 28.2 %all-reduce.3.cloned.1.call-done = bf16[1024,576]{1,0:T(8,128)(2,1)} async-done(((bf16[1024,576]{1,0:T(8,128)(2,1)}), bf16[1024,576]{1,0:T(8,128)(2,1)}) %all-reduce.3.cloned.1.call-update) | async-done | bytes 1179664 | tf_op jit(solution)/shard_map/psum | solution.py:83
  513.9 2.7 copy.95
  516.6 0.0 copy-done.1
  (2 shorter events, 0.1 us)
Async XLA Ops:
  7.2 197.1 %copy-start = (bf16[16,32,128]{2,1,0:T(8,128)(2,1)S(1)}, bf16[16,32,128]{2,1,0:T(8,128)(2,1)}, u32[]{:S(2)}) copy-start(bf16[16,32,128]{2,1,0:T(8,128)(2,1)} %param.13) | copy-start | bytes 393220
  7.2 104.7 %all-gather.5.cloned.1.call-start = ((), (), s32[]{:S(2)}) async-start(), calls=%async_computation.4 | async-start | bytes 4259840 | tf_op jit(solution)/shard_map/all_gather | solution.py:24
  9.3 22.5 %all-to-all-start = ((s32[64,1,1]{2,1,0:T(1,128)}), s32[64,1,1]{2,1,0:T(1,128)S(1)}, u32[]{:S(2)}, u32[]{:S(2)}) async-start(s32[64,1,1]{2,1,0:T(1,128)} %copy.80), calls=%async_computation | async-start | bytes 65536 | tf_op jit(solution)/shard_map/all_to_all | solution.py:29
  37.6 6.6 %copy-start.7 = (s32[16,32]{1,0:T(8,128)S(1)}, s32[16,32]{1,0:T(8,128)}, u32[]{:S(2)}) copy-start(s32[16,32]{1,0:T(8,128)} %param.14) | copy-start | bytes 6148
  37.6 7.3 %copy-start.6 = (bf16[16,32,64]{2,1,0:T(8,128)(2,1)S(1)}, bf16[16,32,64]{2,1,0:T(8,128)(2,1)}, u32[]{:S(2)}) copy-start(bf16[16,32,64]{2,1,0:T(8,128)(2,1)} %param.9) | copy-start | bytes 196612
  37.6 167.9 %all-to-all-start.1 = ((bf16[64,1,64,576]{3,2,1,0:T(8,128)(2,1)}), bf16[64,1,64,576]{3,2,1,0:T(8,128)(2,1)}, u32[]{:S(2)}, u32[]{:S(2)}) async-start(bf16[64,1,64,576]{3,2,1,0:T(8,128)(2,1)} %bitcast.47), calls=%async_computation.1 | async-start | bytes 10485760 | tf_op jit(solution)/shard_map/all_to_all | solution.py:31
  43.5 154.1 %all-gather.3.cloned.1.call-start = ((), (), s32[]{:S(2)}) async-start(), calls=%async_computation.3 | async-start | bytes 4259840 | tf_op jit(solution)/shard_map/all_gather | solution.py:23
  117.0 86.5 %copy-start.5 = (bf16[16,32,128]{2,1,0:T(8,128)(2,1)S(1)}, bf16[16,32,128]{2,1,0:T(8,128)(2,1)}, u32[]{:S(2)}) copy-start(bf16[16,32,128]{2,1,0:T(8,128)(2,1)} %param.8) | copy-start | bytes 393220
  197.6 6.7 %copy-start.2 = (bf16[4,8,512,128]{3,2,1,0:T(8,128)(2,1)S(1)}, bf16[4,8,512,128]{3,2,1,0:T(8,128)(2,1)}, u32[]{:S(2)}) copy-start(bf16[4,8,512,128]{3,2,1,0:T(8,128)(2,1)} %copy.102) | copy-start | bytes 12582916
  201.5 2.1 copy-start.3
  320.4 112.2 %all-to-all-start.2 = ((bf16[64,2,18432]{2,1,0:T(2,128)(2,1)}), bf16[64,2,18432]{2,1,0:T(2,128)(2,1)}, u32[]{:S(2)}, u32[]{:S(2)}) async-start(bf16[64,2,18432]{2,1,0:T(2,128)(2,1)} %reshape.84), calls=%async_computation.2 | async-start | bytes 9437184 | tf_op jit(solution)/shard_map/all_to_all | solution.py:70
  326.9 186.9 %all-reduce.3.cloned.1.call-start = ((), (), s32[]{:S(2)}) async-start(), calls=%async_computation.5 | async-start | bytes 2621440 | tf_op jit(solution)/shard_map/psum | solution.py:83
  478.8 5.0 copy-start.4
  479.5 37.1 %copy-start.1 = (bf16[16,32,128]{2,1,0:T(8,128)(2,1)S(1)}, bf16[16,32,128]{2,1,0:T(8,128)(2,1)}, u32[]{:S(2)}) copy-start(bf16[16,32,128]{2,1,0:T(8,128)(2,1)} %param.13) | copy-start | bytes 393220
Sparse Core Ops, SparseCore 0:
  10.8 101.0 all-gather.4
  114.7 82.8 all-gather.2
  464.1 49.7 all-reduce.2
where the time goes:
time: 529 us; the launch traced here: 523 us
  waiting for transfers between devices  283 us (53%)
  matrix products  84 us (16%)
  local copies, waits for them, and re-layouts  83.7 us (16%)
  other arithmetic  32.5 us (6%)
  starting transfers between devices  26.4 us (5%)
  between operations  14.1 us (3%)
    all_to_all x1, waiting for transfers between devices, local(): lax.all_to_all(dkeys.reshape(peers, per_peer, BLOCK_LEN * width).astype(j...  98.3 us
    all_gather x1, waiting for transfers between devices, local(): lax.all_gather(w_uk, 'seq', axis=1, tiled=True)  80.6 us
    all_gather x1, waiting for transfers between devices, local(): lax.all_gather(w_uv, 'seq', axis=1, tiled=True)  66.9 us
    unnamed x25, local copies, waits for them, and re-layouts  45.4 us
    convert_element_type x1, other arithmetic, local(): dkeys.reshape(peers, per_peer, BLOCK_LEN * width).astype(jnp.bfloat16)  29.9 us
    convert_element_type x3, local copies, waits for them, and re-layouts, local(): dkeys.reshape(peers, per_peer, BLOCK_LEN * width).astype(jnp.bfloat16)  29.9 us
    psum x1, waiting for transfers between devices, local(): lax.psum(local_grad.astype(jnp.bfloat16), 'grp').astype(jnp.float32)  28.2 us
    dot_general x1, matrix products, local(): jnp.einsum('qht,qhc->tc', dscore, qfull, preferred_element_type=jnp.float32)  18.8 us
  transfers between devices with their start and end apart: 6, of which 5 were waited for; matrix products, arithmetic and copies ran while one was open for 9% of the time, Pallas kernels for 0%

commit v1 on v0

v1 whole, which is shorter than its diff:
```python
import math

import jax
import jax.numpy as jnp
from jax import lax
from jax.experimental import pallas as pl
from jax.experimental.pallas import tpu as pltpu
from jax.sharding import PartitionSpec as P

MESH = pl.DeviceIdType.MESH
BF = jnp.bfloat16
F32 = jnp.float32
ZN, YN, XN = 8, 4, 4
ORDER = (0, 1, 7, 2, 6, 3, 5, 4)
NEG = -1e30


def rcopy(src, dst, ssem, rsem, seq, grp):
    return pltpu.make_async_remote_copy(
        src_ref=src, dst_ref=dst, send_sem=ssem, recv_sem=rsem,
        device_id=(seq, grp), device_id_type=MESH,
    )


def place():
    si = lax.axis_index("seq")
    g = lax.axis_index("grp")
    c = lax.rem(si, 2)
    y = lax.rem(si // 2, YN)
    z = si // (2 * YN)
    return si, g, z, y, c


def sid(z, y, c):
    return (lax.rem(z, ZN) * YN + lax.rem(y, YN)) * 2 + c


def peers():
    return [(dz, dy, dc) for dz in ORDER for dy in range(YN) for dc in range(2) if (dz, dy, dc) != (0, 0, 0)]


def fetch_kernel(wsh, cache, slot, keys, wall, m_ref,
                 table, send, zs, zr, ys, yr, ss, sr, ixs, ixr, as_, ar, xs, xr, loc):
    si, g, z, y, c = place()
    zp, zm = sid(z + 1, y, c), sid(z + 7, y, c)
    yp, ym = sid(z, y + 1, c), sid(z, y + 3, c)
    sib = sid(z, y, 1 - c)
    gr, gl = lax.rem(g + 1, XN), lax.rem(g + 3, XN)
    sends = []

    def go(cp):
        cp.start()
        sends.append(cp)

    def src_of(a, b):
        return sid(z + (ZN - a), y + (YN - b), c)

    def half(ref, h):
        return ref.at[pl.ds(32 * h, 32)]

    own = pltpu.make_async_copy(wsh, wall.at[si], loc.at[0])
    own.start()
    mine = pltpu.make_async_copy(slot, table.at[si], loc.at[1])
    mine.start()
    for (dz, dy, dc) in peers():
        to = sid(z + dz, y + dy, lax.rem(c + dc, 2))
        go(rcopy(slot, table.at[si], ixs.at[dz, dy, dc], ixr.at[dz, dy, dc], to, g))
    go(rcopy(wsh, wall.at[si], zs.at[0, 0], zr.at[0, 0], zp, g))
    go(rcopy(wsh, wall.at[si], zs.at[1, 0], zr.at[1, 0], zm, g))

    def y_send(a):
        s = src_of(a, 0)
        ref = wsh if a == 0 else wall.at[s]
        go(rcopy(ref, wall.at[s], ys.at[a, 0, 0], yr.at[a, 0, 0], yp, g))
        go(rcopy(ref, wall.at[s], ys.at[a, 1, 0], yr.at[a, 1, 0], ym, g))
        go(rcopy(ref, wall.at[s], ss.at[a, 0], sr.at[a, 0], sib, g))

    def z_step(k):
        for d in range(2):
            a = k if d == 0 else ZN - k
            s = src_of(a, 0)
            ref = wall.at[s] if k < 4 else half(wall.at[s], d)
            to = zp if d == 0 else zm
            rcopy(ref, ref, zs.at[d, k - 1], zr.at[d, k - 1], to, g).wait_recv()
            if k < 4:
                nxt = wall.at[s] if k < 3 else half(wall.at[s], d)
                go(rcopy(nxt, nxt, zs.at[d, k], zr.at[d, k], to, g))

    def y_near(a):
        for d in range(2):
            s = src_of(a, 1 if d == 0 else 3)
            ref = wall.at[s]
            to = yp if d == 0 else ym
            rcopy(ref, ref, ys.at[a, d, 0], yr.at[a, d, 0], to, g).wait_recv()
            h = half(ref, d)
            go(rcopy(h, h, ys.at[a, d, 1], yr.at[a, d, 1], to, g))
            b = 1 if d == 0 else 3
            go(rcopy(ref, ref, ss.at[a, b], sr.at[a, b], sib, g))

    def y_far(a):
        s = src_of(a, 2)
        for d in range(2):
            h = half(wall.at[s], d)
            rcopy(h, h, ys.at[a, d, 1], yr.at[a, d, 1], yp if d == 0 else ym, g).wait_recv()
        go(rcopy(wall.at[s], wall.at[s], ss.at[a, 2], sr.at[a, 2], sib, g))

    y_send(0)
    z_step(1)
    y_send(1)
    y_send(7)
    mine.wait()
    for (dz, dy, dc) in peers():
        s = sid(z + (ZN - dz), y + (YN - dy), lax.rem(c + dc, 2))
        rcopy(slot, table.at[s], ixs.at[dz, dy, dc], ixr.at[dz, dy, dc], s, g).wait_recv()

    lane = lax.broadcasted_iota(jnp.int32, (8, 128), 1)
    col = lax.broadcasted_iota(jnp.int32, (8, 256), 1)
    row = lax.broadcasted_iota(jnp.int32, (8, 256), 0)
    colb, colt = col // 16, lax.rem(col, 16)

    def build(r, carry):
        v = jnp.sum(jnp.where(lane == si, table[r], 0), axis=1, keepdims=True)
        top = jnp.where((colb == v) & (colt == row), 1.0, 0.0)
        bot = jnp.where((colb == v) & (colt == row + 8), 1.0, 0.0)
        m_ref[r] = jnp.concatenate([top, bot], axis=0).astype(BF)
        return carry

    lax.fori_loop(0, 64, build, 0)
    cq = cache[:, g].reshape(256, 576)

    def pick(i, carry):
        rows = pl.ds(8 * i, 8)
        got = jnp.dot(m_ref[rows].reshape(128, 256), cq, preferred_element_type=F32)
        send[rows] = got.astype(BF).reshape(8, 16, 576)
        return carry

    lax.fori_loop(0, 8, pick, 0)
    z_step(2)
    y_send(2)
    y_send(6)
    keys[si, g] = send[si]
    for (dz, dy, dc) in peers():
        to = sid(z + dz, y + dy, lax.rem(c + dc, 2))
        go(rcopy(send.at[to], keys.at[si, g], as_.at[dz, dy, dc], ar.at[dz, dy, dc], to, g))
    z_step(3)
    y_send(3)
    y_send(5)
    z_step(4)
    y_send(4)

    def x_part(i, who, d, far):
        base = 8 * lax.rem(z + ZN - i, ZN)
        if far:
            return keys.at[pl.ds(base + 4 * d, 4), who]
        return keys.at[pl.ds(base, 8), who]

    def x_start(i):
        for dy in range(YN):
            for dc in range(2):
                if (i, dy, dc) != (0, 0, 0):
                    s = sid(z + (ZN - i), y + (YN - dy), lax.rem(c + dc, 2))
                    rcopy(send.at[s], keys.at[s, g], as_.at[i, dy, dc], ar.at[i, dy, dc], s, g).wait_recv()
        ref = x_part(i, g, 0, False)
        go(rcopy(ref, ref, xs.at[i, 0, 0], xr.at[i, 0, 0], si, gr))
        go(rcopy(ref, ref, xs.at[i, 1, 0], xr.at[i, 1, 0], si, gl))

    def x_fwd(i):
        for d in range(2):
            who = gl if d == 0 else gr
            to = gr if d == 0 else gl
            ref = x_part(i, who, d, False)
            rcopy(ref, ref, xs.at[i, d, 0], xr.at[i, d, 0], si, to).wait_recv()
            h = x_part(i, who, d, True)
            go(rcopy(h, h, xs.at[i, d, 1], xr.at[i, d, 1], si, to))

    def x_done(i):
        who = lax.rem(g + 2, XN)
        for d in range(2):
            h = x_part(i, who, d, True)
            rcopy(h, h, xs.at[i, d, 1], xr.at[i, d, 1], si, gr if d == 0 else gl).wait_recv()

    for t in range(10):
        if t < 8:
            y_near(ORDER[t])
            x_start(ORDER[t])
        if 1 <= t < 9:
            y_far(ORDER[t - 1])
            x_fwd(ORDER[t - 1])
        if t >= 2:
            x_done(ORDER[t - 2])
    own.wait()
    for a in range(8):
        for b in range(4):
            s = sid(z + (ZN - a), y + (YN - b), 1 - c)
            rcopy(wall.at[s], wall.at[s], ss.at[a, b], sr.at[a, b], sib, g).wait_recv()
    for cp in sends:
        cp.wait_send()


def vm():
    return pl.BlockSpec(memory_space=pltpu.VMEM)


def fetch(wsh, cache, slot):
    dma = pltpu.SemaphoreType.DMA
    return pl.pallas_call(
        fetch_kernel,
        name="fetch",
        out_shape=(
            jax.ShapeDtypeStruct((64, 4, 16, 576), BF),
            jax.ShapeDtypeStruct((64, 64, 8, 128), BF),
            jax.ShapeDtypeStruct((64, 16, 256), BF),
        ),
        in_specs=[vm()] * 3,
        out_specs=(vm(),) * 3,
        scratch_shapes=[
            pltpu.VMEM((64, 8, 128), jnp.int32),
            pltpu.VMEM((64, 16, 576), BF),
            dma((2, 4)), dma((2, 4)),
            dma((8, 2, 2)), dma((8, 2, 2)),
            dma((8, 4)), dma((8, 4)),
            dma((8, 4, 2)), dma((8, 4, 2)),
            dma((8, 4, 2)), dma((8, 4, 2)),
            dma((8, 2, 2)), dma((8, 2, 2)),
            dma((2,)),
        ],
        compiler_params=pltpu.CompilerParams(has_side_effects=True),
    )(wsh, cache, slot)


def give_kernel(dk, m_ref, out, fl, fr, nl, nr, tol, tor, send, got,
                fs, fr_, ns, nr_, as_, ar, gs, gr_):
    si, g, z, y, c = place()
    gr, gl, go2 = lax.rem(g + 1, XN), lax.rem(g + 3, XN), lax.rem(g + 2, XN)
    sends = []

    def go(cp):
        cp.start()
        sends.append(cp)

    def lo(i):
        return pl.ds(8 * lax.rem(z + i, ZN), 4)

    def hi(i):
        return pl.ds(8 * lax.rem(z + i, ZN) + 4, 4)

    for i in ORDER:
        go(rcopy(dk.at[lo(i), go2], fl.at[i], fs.at[i, 0], fr_.at[i, 0], si, gr))
        go(rcopy(dk.at[hi(i), go2], fr.at[i], fs.at[i, 1], fr_.at[i, 1], si, gl))
        go(rcopy(dk.at[hi(i), gr], nl.at[hi(i)], ns.at[i, 0, 0], nr_.at[i, 0, 0], si, gr))
        go(rcopy(dk.at[lo(i), gl], nr.at[lo(i)], ns.at[i, 1, 0], nr_.at[i, 1, 0], si, gl))

    def combine(i):
        rcopy(fl.at[i], fl.at[i], fs.at[i, 0], fr_.at[i, 0], si, gr).wait_recv()
        tor[i] = (dk[lo(i), gr].astype(F32) + fl[i].astype(F32)).astype(BF)
        rcopy(fr.at[i], fr.at[i], fs.at[i, 1], fr_.at[i, 1], si, gl).wait_recv()
        tol[i] = (dk[hi(i), gl].astype(F32) + fr[i].astype(F32)).astype(BF)
        go(rcopy(tor.at[i], nl.at[lo(i)], ns.at[i, 0, 1], nr_.at[i, 0, 1], si, gr))
        go(rcopy(tol.at[i], nr.at[hi(i)], ns.at[i, 1, 1], nr_.at[i, 1, 1], si, gl))

    def owner(i):
        rcopy(nl.at[hi(i)], nl.at[hi(i)], ns.at[i, 0, 0], nr_.at[i, 0, 0], si, gr).wait_recv()
        rcopy(nr.at[lo(i)], nr.at[lo(i)], ns.at[i, 1, 0], nr_.at[i, 1, 0], si, gl).wait_recv()
        rcopy(nl.at[lo(i)], nl.at[lo(i)], ns.at[i, 0, 1], nr_.at[i, 0, 1], si, gr).wait_recv()
        rcopy(nr.at[hi(i)], nr.at[hi(i)], ns.at[i, 1, 1], nr_.at[i, 1, 1], si, gl).wait_recv()
        al = pl.ds(8 * lax.rem(z + i, ZN), 8)
        send[al] = (dk[al, g].astype(F32) + nl[al].astype(F32) + nr[al].astype(F32)).astype(BF)
        for dy in range(YN):
            for dc in range(2):
                if (i, dy, dc) != (0, 0, 0):
                    to = sid(z + i, y + dy, lax.rem(c + dc, 2))
                    go(rcopy(send.at[to], got.at[si], as_.at[i, dy, dc], ar.at[i, dy, dc], to, g))

    for t in range(9):
        if t < 8:
            combine(ORDER[t])
        if t >= 1:
            owner(ORDER[t - 1])
    got[si] = send[si]
    for (dz, dy, dc) in peers():
        s = sid(z + (ZN - dz), y + (YN - dy), lax.rem(c + dc, 2))
        rcopy(got.at[s], got.at[s], as_.at[dz, dy, dc], ar.at[dz, dy, dc], s, g).wait_recv()
    acc = lax.dot_general(m_ref[...].reshape(1024, 256), got[...].reshape(1024, 576),
                          (((0,), (0,)), ((), ())), preferred_element_type=F32)
    out[:, g] = acc.astype(BF).reshape(16, 16, 576)
    ref = out.at[:, g]
    go(rcopy(ref, ref, gs.at[0, 0], gr_.at[0, 0], si, gr))
    go(rcopy(ref, ref, gs.at[1, 0], gr_.at[1, 0], si, gl))
    for d in range(2):
        who, to = (gl, gr) if d == 0 else (gr, gl)
        ref = out.at[:, who]
        rcopy(ref, ref, gs.at[d, 0], gr_.at[d, 0], si, to).wait_recv()
        h = out.at[pl.ds(8 * d, 8), who]
        go(rcopy(h, h, gs.at[d, 1], gr_.at[d, 1], si, to))
    for d in range(2):
        h = out.at[pl.ds(8 * d, 8), go2]
        rcopy(h, h, gs.at[d, 1], gr_.at[d, 1], si, gr if d == 0 else gl).wait_recv()
    for cp in sends:
        cp.wait_send()


def give(dk, m):
    dma = pltpu.SemaphoreType.DMA
    return pl.pallas_call(
        give_kernel,
        name="give",
        out_shape=jax.ShapeDtypeStruct((16, 4, 16, 576), BF),
        in_specs=[vm()] * 2,
        out_specs=vm(),
        scratch_shapes=[
            pltpu.VMEM((8, 4, 16, 576), BF), pltpu.VMEM((8, 4, 16, 576), BF),
            pltpu.VMEM((64, 16, 576), BF), pltpu.VMEM((64, 16, 576), BF),
            pltpu.VMEM((8, 4, 16, 576), BF), pltpu.VMEM((8, 4, 16, 576), BF),
            pltpu.VMEM((64, 16, 576), BF), pltpu.VMEM((64, 16, 576), BF),
            dma((8, 2)), dma((8, 2)),
            dma((8, 2, 2)), dma((8, 2, 2)),
            dma((8, 4, 2)), dma((8, 4, 2)),
            dma((2, 2)), dma((2, 2)),
        ],
        compiler_params=pltpu.CompilerParams(has_side_effects=True),
    )(dk, m)


NT = (((1,), (1,)), ((), ()))
TN = (((0,), (0,)), ((), ()))
SCALE = 1.0 / math.sqrt(192.0)
TJ = 512


def attend_kernel(qn, qr, do, keys, wall, bias, attn, dqn, dqr, dk,
                  qf, dol, e_ref, dp_ref, mj_ref, dqt, ot, gsum, ol, dql):
    rep = jnp.where(
        lax.broadcasted_iota(jnp.int32, (128, 512), 1) // 4 == lax.broadcasted_iota(jnp.int32, (128, 512), 0), 1.0, 0.0
    ).astype(BF)
    lb_mask = lax.rem(lax.broadcasted_iota(jnp.int32, (64, 512), 1), 4) == (
        lax.broadcasted_iota(jnp.int32, (64, 512), 0) // 16
    )

    def weight(i):
        return wall[:, i].astype(F32).reshape(512, 128).astype(BF)

    def project(h, carry):
        rows = pl.ds(pl.multiple_of(16 * h, 16), 16)
        wide = jnp.dot(qn[h], rep, preferred_element_type=F32)
        wide = jnp.where(lb_mask, jnp.concatenate([wide] * 4, axis=0), 0.0).astype(BF)
        lat = jnp.dot(wide, weight(h), preferred_element_type=F32)
        qf[rows, 0:512] = jnp.concatenate([lat[16 * b:16 * b + 16] for b in range(4)], axis=1).astype(BF)
        dol[rows, :] = lax.dot_general(do[h], weight(32 + h), NT, preferred_element_type=F32).astype(BF)
        return carry

    lax.fori_loop(0, 32, project, 0)
    qf[:, 512:576] = qr[...]

    def first(j, carry):
        m, l, d = carry
        kj = keys[pl.ds(pl.multiple_of(TJ * j, TJ), TJ), :]
        s = lax.dot_general(kj, qf[...], NT, preferred_element_type=F32) * SCALE
        b = bias[pl.ds(pl.multiple_of(8 * j, 8), 8), :]
        s = (s.reshape(8, 64, 512) + b[:, None, :]).reshape(TJ, 512)
        mn = jnp.maximum(m, jnp.max(s, axis=0, keepdims=True))
        e = jnp.exp(s - mn)
        dp = lax.dot_general(kj[:, :512], dol[...], NT, preferred_element_type=F32)
        e_ref[j] = e
        dp_ref[j] = dp
        mj_ref[j] = mn
        al = jnp.exp(m - mn)
        return (mn, l * al + jnp.sum(e, axis=0, keepdims=True), d * al + jnp.sum(e * dp, axis=0, keepdims=True))

    one = jnp.zeros((1, 512), F32)
    m, l, d = lax.fori_loop(0, 8, first, (one + NEG, one, one))
    inv = 1.0 / l
    delta = d * inv
    dqt[...] = jnp.zeros_like(dqt)
    ot[...] = jnp.zeros_like(ot)

    def second(j, carry):
        rows = pl.ds(pl.multiple_of(TJ * j, TJ), TJ)
        kj = keys[rows, :]
        p = e_ref[j] * (jnp.exp(mj_ref[j] - m) * inv)
        pb = p.astype(BF)
        ds = (p * (dp_ref[j] - delta) * SCALE).astype(BF)
        gk = jnp.dot(ds, qf[...], preferred_element_type=F32)
        gv = jnp.dot(pb, dol[...], preferred_element_type=F32)
        dk[rows, 0:512] = (gk[:, :512] + gv).astype(BF)
        dk[rows, 512:576] = gk[:, 512:].astype(BF)
        dqt[...] += lax.dot_general(kj, ds, TN, preferred_element_type=F32)
        ot[...] += lax.dot_general(kj[:, :512], pb, TN, preferred_element_type=F32)
        return carry

    lax.fori_loop(0, 8, second, 0)
    ol[...] = jnp.transpose(ot[...]).astype(BF)
    dql[...] = jnp.transpose(dqt[0:512, :]).astype(BF)
    dqr[...] = jnp.transpose(dqt[512:576, :]).astype(BF)

    def finish(h, carry):
        rows = pl.ds(pl.multiple_of(16 * h, 16), 16)
        attn[h] = jnp.dot(ol[rows, :], weight(32 + h), preferred_element_type=F32).astype(BF)
        x = dql[rows, :]
        x = jnp.concatenate([x[:, 128 * b:128 * b + 128] for b in range(4)], axis=0)
        r = lax.dot_general(x, weight(h), NT, preferred_element_type=F32)
        r = jnp.where(lb_mask, r, 0.0)
        gsum[rows, :] = r[0:16] + r[16:32] + r[32:48] + r[48:64]
        return carry

    lax.fori_loop(0, 32, finish, 0)
    gs = gsum[...]
    g0 = gs.astype(BF)
    r1 = gs - g0.astype(F32)
    g1 = r1.astype(BF)
    g2 = (r1 - g1.astype(F32)).astype(BF)
    acc = lax.dot_general(g0, rep, NT, preferred_element_type=F32)
    acc += lax.dot_general(g1, rep, NT, preferred_element_type=F32)
    acc += lax.dot_general(g2, rep, NT, preferred_element_type=F32)
    dqn[...] = acc.astype(BF)


def attend(qn, qr, do, keys, wall, bias):
    return pl.pallas_call(
        attend_kernel,
        name="attend",
        out_shape=(
            jax.ShapeDtypeStruct((32, 16, 128), BF),
            jax.ShapeDtypeStruct((512, 128), BF),
            jax.ShapeDtypeStruct((512, 64), BF),
            jax.ShapeDtypeStruct((4096, 576), BF),
        ),
        in_specs=[vm()] * 6,
        out_specs=(vm(),) * 4,
        scratch_shapes=[
            pltpu.VMEM((512, 576), BF), pltpu.VMEM((512, 512), BF),
            pltpu.VMEM((8, TJ, 512), F32), pltpu.VMEM((8, TJ, 512), F32),
            pltpu.VMEM((8, 1, 512), F32),
            pltpu.VMEM((576, 512), F32), pltpu.VMEM((512, 512), F32),
            pltpu.VMEM((512, 512), F32), pltpu.VMEM((512, 512), BF), pltpu.VMEM((512, 512), BF),
        ],
        compiler_params=pltpu.CompilerParams(vmem_limit_bytes=62 << 20),
    )(qn, qr, do, keys, wall, bias)


def local(q_nope, q_rope, cache, w_uk, w_uv, d_out, sel, slot_blocks):
    wsh = jnp.concatenate([w_uk.reshape(32, 8, 128), w_uv.reshape(32, 8, 128)], axis=0)
    slot = jnp.pad(jnp.broadcast_to(slot_blocks, (8, 64)), ((0, 0), (0, 64)))
    keys, wall, m = fetch(wsh, cache.reshape(16, 4, 16, 576), slot)
    qn = jnp.transpose(q_nope, (1, 0, 2))
    do = jnp.transpose(d_out, (1, 0, 2))
    qr = jnp.transpose(q_rope, (1, 0, 2)).reshape(512, 64)
    chosen = jnp.any(sel[:, :, None] == jnp.arange(64, dtype=jnp.int32)[None, None, :], axis=1)
    bias = jnp.tile(jnp.where(chosen, 0.0, NEG).astype(F32).T, (1, 32))
    attn, dqn, dqr, dk = attend(qn, qr, do, keys.reshape(4096, 576), wall, bias)
    dc = give(dk.reshape(64, 4, 16, 576), m)
    return (
        jnp.transpose(attn, (1, 0, 2)),
        jnp.transpose(dqn.reshape(32, 16, 128), (1, 0, 2)),
        jnp.transpose(dqr.reshape(32, 16, 64), (1, 0, 2)),
        dc.astype(F32).reshape(1024, 576),
    )


def solution(mesh):
    return jax.shard_map(
        local,
        mesh=mesh,
        in_specs=(
            P("seq", "grp", None),
            P("seq", "grp", None),
            P("seq", None),
            P("grp", "seq"),
            P("grp", "seq"),
            P("seq", "grp", None),
            P("seq", None),
            P("seq", None),
        ),
        out_specs=(
            P("seq", "grp", None),
            P("seq", "grp", None),
            P("seq", "grp", None),
            P("seq", None),
        ),
        check_vma=False,
    )
```

time: 529 us -> 290 us (0.55)
  waiting for transfers between devices: 283 us -> 0 us
  Pallas kernels: 0 us -> 270 us
  matrix products: 84 us -> 0 us
  local copies, waits for them, and re-layouts: 83.7 us -> 15.4 us
  other arithmetic: 32.5 us -> 3 us
  starting transfers between devices: 26.4 us -> 0 us
  between operations: 14.1 us -> 0.68 us
    pallas_call x0 -> x3, Pallas kernels: none -> 270 us  [the longest x1 126 us: fetch(): pl.pallas_call(fetch_kernel, name='fetch', out_shape=(jax.ShapeDtypeStruc...]
    all_gather x2 -> x0, waiting for transfers between devices: 148 us -> none  [the longest x1 80.6 us: local(): lax.all_gather(w_uk, 'seq', axis=1, tiled=True)]
    all_to_all x3 -> x0, waiting for transfers between devices: 106 us -> none  [the longest x1 98.3 us: local(): lax.all_to_all(dkeys.reshape(peers, per_peer, BLOCK_LEN * width).astype(j...]
    dot_general x10 -> x0, matrix products: 73.3 us -> none  [the longest x1 18.8 us: local(): jnp.einsum('qht,qhc->tc', dscore, qfull, preferred_element_type=jnp.float32)]
    unnamed x25 -> x7, local copies, waits for them, and re-layouts: 45.4 us -> 6.72 us
    convert_element_type x1 -> x0, other arithmetic: 29.9 us -> none  [local(): dkeys.reshape(peers, per_peer, BLOCK_LEN * width).astype(jnp.bfloat16)]
    convert_element_type x3 -> x0, local copies, waits for them, and re-layouts: 29.9 us -> none  [local(): dkeys.reshape(peers, per_peer, BLOCK_LEN * width).astype(jnp.bfloat16)]
    psum x1 -> x0, waiting for transfers between devices: 28.2 us -> none  [local(): lax.psum(local_grad.astype(jnp.bfloat16), 'grp').astype(jnp.float32)]
  transfers between devices with their start and end apart: 6 -> 0, of which waited for: 5 -> 0; matrix products, arithmetic and copies ran while one was open for 9% -> 0% of each run, Pallas kernels for 0% -> 0%
where the time goes in v1:
time: 290 us; the launch traced here: 289 us
  Pallas kernels  270 us (93%)
  local copies, waits for them, and re-layouts  15.4 us (5%)
  other arithmetic  3 us (1%)
    pallas_call x1, Pallas kernels, fetch(): pl.pallas_call(fetch_kernel, name='fetch', out_shape=(jax.ShapeDtypeStruc...  126 us
    pallas_call x1, Pallas kernels, give(): pl.pallas_call(give_kernel, name='give', out_shape=jax.ShapeDtypeStruct((...  101 us
    pallas_call x1, Pallas kernels, attend(): pl.pallas_call(attend_kernel, name='attend', out_shape=(jax.ShapeDtypeStr...  43.1 us
    unnamed x7, local copies, waits for them, and re-layouts  6.72 us

profile of v1, /device:TPU:1, one launch (start us, length us, event | category | flops | bytes accessed | tf_op | source)
XLA Modules:
  0.0 289.5 jit_solution(254080503718811102)
XLA Ops:
  0.6 0.0 copy-start
  0.6 0.8 pad.6
  1.4 0.8 fusion
  2.2 0.6 pad.7.slot
  2.8 0.8 copy.38
  3.7 0.9 copy.39
  4.6 0.7 pad_maximum_fusion.wsh
  5.2 1.6 copy.30
  6.8 0.8 copy.33.bias
  7.6 1.8 copy_bitcast_fusion.2
  9.4 0.0 copy-done
  9.4 1.4 copy.32
  10.8 126.3 %fetch.1 = (bf16[64,4,16,576]{3,2,1,0:T(8,128)(2,1)}, bf16[64,64,8,128]{3,2,1,0:T(8,128)(2,1)}, bf16[64,16,256]{2,1,0:T(8,128)(2,1)}) custom-call(bf16[64,8,128]{2,1,0:T(8,128)(2,1)} %pad_maximum_fusion.wsh, bf16[16,4,16,576]{3,2,1,0:T(8,128)(2,1)} %bitcast.31, s32[8,128]{1,0:T(8,128)} %pad.7.slot), custom_call_target="tpu_custom_call" | custom-call | tf_op jit(solution)/shard_map/fetch/pallas_call | solution.py:206
  137.1 43.1 %attend.1 = (bf16[32,16,128]{2,1,0:T(8,128)(2,1)}, bf16[512,128]{1,0:T(8,128)(2,1)}, bf16[512,64]{1,0:T(8,128)(2,1)}, bf16[4096,576]{1,0:T(8,128)(2,1)}) custom-call(bf16[32,16,128]{2,1,0:T(8,128)(2,1)} %get-tuple-element.31.qn, bf16[512,64]{1,0:T(8,128)(2,1)} %bitcast.33, bf16[32,16,128]{2,1,0:T(8,128)(2,1)} %get-tuple-element.30.do, ...), custom_call_target="tpu_custom_call" | custom-call | tf_op jit(solution)/shard_map/attend/pallas_call | solution.py:418
  180.2 1.6 copy.36
  181.8 1.6 copy.45
  183.4 1.6 copy.44
  185.0 101.0 %give.1 = bf16[16,4,16,576]{3,2,1,0:T(8,128)(2,1)} custom-call(bf16[64,4,16,576]{3,2,1,0:T(8,128)(2,1)} %bitcast.30, bf16[64,16,256]{2,1,0:T(8,128)(2,1)} %get-tuple-element.17.m_ref), custom_call_target="tpu_custom_call" | custom-call | tf_op jit(solution)/shard_map/give/pallas_call | solution.py:304
  286.0 1.5 bitcast_convert_fusion
  287.5 2.0 copy.37
  (2 shorter events, 0.0 us)
Async XLA Ops:
  0.6 8.8 %copy-start = (bf16[1024,576]{0,1:T(8,128)(2,1)S(1)}, bf16[1024,576]{0,1:T(8,128)(2,1)}, u32[]{:S(2)}) copy-start(bf16[1024,576]{0,1:T(8,128)(2,1)} %param.10) | copy-start | bytes 3538948

commit v2 on v0

v2 whole, which is shorter than its diff:
```python
import math

import jax
import jax.numpy as jnp
from jax import lax
from jax.experimental import pallas as pl
from jax.experimental.pallas import tpu as pltpu
from jax.sharding import PartitionSpec as P

MESH = pl.DeviceIdType.MESH
BF = jnp.bfloat16
F32 = jnp.float32
ZN, YN, XN = 8, 4, 4
ORDER = (0, 5, 2, 7, 4, 1, 6, 3)
NEG = -1e30
ORDER_W = (0, 1, 7, 2, 6, 3, 5, 4)


def rcopy(src, dst, ssem, rsem, seq, grp):
    return pltpu.make_async_remote_copy(
        src_ref=src, dst_ref=dst, send_sem=ssem, recv_sem=rsem,
        device_id=(seq, grp), device_id_type=MESH,
    )


def place():
    si = lax.axis_index("seq")
    g = lax.axis_index("grp")
    c = lax.rem(si, 2)
    y = lax.rem(si // 2, YN)
    z = si // (2 * YN)
    return si, g, z, y, c


def sid(z, y, c):
    return (lax.rem(z, ZN) * YN + lax.rem(y, YN)) * 2 + c


def peers():
    return [(dz, dy, dc) for dz in ORDER for dy in range(YN) for dc in range(2) if (dz, dy, dc) != (0, 0, 0)]


NT = (((1,), (1,)), ((), ()))
TN = (((0,), (0,)), ((), ()))
SCALE = 1.0 / math.sqrt(192.0)


def step_of(t):
    return lax.rem(5 * t, 8)


def whole_kernel(qn_in, qr_in, do_in, cache, wk_in, wv_in, sel, slot,
                 attn, dqn, dqr, out,
                 wsh, wall, table, m_ref, send, keys,
                 qn, do, qf, dol, bias, e_ref, dp_ref, mj_ref, dk,
                 dqt, ot, ol, dql, at_t, fl, fr, nl, nr, tol, tor, got,
                 zs, zr, ys, yr, ss, sr, ixs, ixr, as_, ar, xs, xr, loc,
                 fs, fq, ns, nq, bs, br, gs, gq):
    si, g, z, y, c = place()
    zp, zm = sid(z + 1, y, c), sid(z + 7, y, c)
    yp, ym = sid(z, y + 1, c), sid(z, y + 3, c)
    sib = sid(z, y, 1 - c)
    gr, gl, gf = lax.rem(g + 1, XN), lax.rem(g + 3, XN), lax.rem(g + 2, XN)
    barrier = pltpu.get_barrier_semaphore()
    for (dz, dy, dc) in peers():
        pl.semaphore_signal(barrier, inc=1, device_id=(sid(z + dz, y + dy, lax.rem(c + dc, 2)), g), device_id_type=MESH)
    pl.semaphore_signal(barrier, inc=1, device_id=(si, gr), device_id_type=MESH)
    pl.semaphore_signal(barrier, inc=1, device_id=(si, gl), device_id_type=MESH)

    for i, w_in in ((0, wk_in), (32, wv_in)):
        wsh[i:i + 32] = w_in[...].astype(F32).reshape(32, 8, 128).astype(BF)
    pl.semaphore_wait(barrier, 65)

    late = []

    def go(cp):
        cp.start()
        late.append(cp)

    def src_of(a, b):
        return sid(z + (ZN - a), y + (YN - b), c)

    def tiles(ref, kv, h=None):
        if h is None:
            return ref.at[pl.ds(32 * kv, 32)]
        return ref.at[pl.ds(32 * kv + 16 * h, 16)]

    own = pltpu.make_async_copy(wsh, wall.at[si], loc.at[0])
    own.start()
    mine = pltpu.make_async_copy(slot, table.at[si], loc.at[1])
    mine.start()
    go(rcopy(tiles(wsh, 0), tiles(wall.at[si], 0), zs.at[0, 0, 0], zr.at[0, 0, 0], zp, g))
    go(rcopy(tiles(wsh, 0), tiles(wall.at[si], 0), zs.at[0, 1, 0], zr.at[0, 1, 0], zm, g))
    for (dz, dy, dc) in peers():
        to = sid(z + dz, y + dy, lax.rem(c + dc, 2))
        go(rcopy(slot, table.at[si], ixs.at[dz, dy, dc], ixr.at[dz, dy, dc], to, g))
    go(rcopy(tiles(wsh, 1), tiles(wall.at[si], 1), zs.at[1, 0, 0], zr.at[1, 0, 0], zp, g))
    go(rcopy(tiles(wsh, 1), tiles(wall.at[si], 1), zs.at[1, 1, 0], zr.at[1, 1, 0], zm, g))

    def y_send(kv, a):
        s = src_of(a, 0)
        ref = tiles(wsh if a == 0 else wall.at[s], kv)
        dst = tiles(wall.at[s], kv)
        go(rcopy(ref, dst, ys.at[kv, a, 0, 0], yr.at[kv, a, 0, 0], yp, g))
        go(rcopy(ref, dst, ys.at[kv, a, 1, 0], yr.at[kv, a, 1, 0], ym, g))
        go(rcopy(ref, dst, ss.at[kv, a, 0], sr.at[kv, a, 0], sib, g))

    def z_step(kv, k):
        for d in range(2):
            a = k if d == 0 else ZN - k
            s = src_of(a, 0)
            ref = tiles(wall.at[s], kv) if k < 4 else tiles(wall.at[s], kv, d)
            to = zp if d == 0 else zm
            rcopy(ref, ref, zs.at[kv, d, k - 1], zr.at[kv, d, k - 1], to, g).wait_recv()
            if k < 4:
                nxt = tiles(wall.at[s], kv) if k < 3 else tiles(wall.at[s], kv, d)
                go(rcopy(nxt, nxt, zs.at[kv, d, k], zr.at[kv, d, k], to, g))

    def y_near(kv, a):
        for d in range(2):
            b = 1 if d == 0 else 3
            s = src_of(a, b)
            ref = tiles(wall.at[s], kv)
            to = yp if d == 0 else ym
            rcopy(ref, ref, ys.at[kv, a, d, 0], yr.at[kv, a, d, 0], to, g).wait_recv()
            h = tiles(wall.at[s], kv, d)
            go(rcopy(h, h, ys.at[kv, a, d, 1], yr.at[kv, a, d, 1], to, g))
            go(rcopy(ref, ref, ss.at[kv, a, b], sr.at[kv, a, b], sib, g))

    def y_far(kv, a):
        s = src_of(a, 2)
        for d in range(2):
            h = tiles(wall.at[s], kv, d)
            rcopy(h, h, ys.at[kv, a, d, 1], yr.at[kv, a, d, 1], yp if d == 0 else ym, g).wait_recv()
        ref = tiles(wall.at[s], kv)
        go(rcopy(ref, ref, ss.at[kv, a, 2], sr.at[kv, a, 2], sib, g))

    def sib_wait(kv):
        for a in range(8):
            for b in range(4):
                ref = tiles(wall.at[sid(z + (ZN - a), y + (YN - b), 1 - c)], kv)
                rcopy(ref, ref, ss.at[kv, a, b], sr.at[kv, a, b], sib, g).wait_recv()

    y_send(0, 0)
    z_step(0, 1)
    y_send(0, 1)
    y_send(0, 7)
    mine.wait()
    z_step(0, 2)
    y_send(0, 2)
    y_send(0, 6)
    z_step(1, 1)
    z_step(0, 3)
    y_send(0, 3)
    y_send(0, 5)
    z_step(1, 2)
    z_step(0, 4)
    y_send(0, 4)
    z_step(1, 3)
    for (dz, dy, dc) in peers():
        s = sid(z + (ZN - dz), y + (YN - dy), lax.rem(c + dc, 2))
        rcopy(slot, table.at[s], ixs.at[dz, dy, dc], ixr.at[dz, dy, dc], s, g).wait_recv()

    lane = lax.broadcasted_iota(jnp.int32, (1, 64), 1)
    col = lax.broadcasted_iota(jnp.int32, (16, 256), 1)
    row = lax.broadcasted_iota(jnp.int32, (16, 256), 0)
    colb, same = col // 16, lax.rem(col, 16) == row

    def build(i, carry):
        for k in range(8):
            r = 8 * i + k
            v = jnp.sum(jnp.where(lane == si, table[r].astype(F32), 0.0), axis=1, keepdims=True).astype(jnp.int32)
            hit = (colb == jnp.broadcast_to(v, (16, 256))) & same
            m_ref[r] = jnp.where(hit, 1.0, 0.0).astype(BF)
        return carry

    lax.fori_loop(0, 8, build, 0)
    cq = cache[:, g].reshape(256, 576)

    def pick(i, carry):
        rows = pl.ds(8 * i, 8)
        pulled = jnp.dot(m_ref[rows].reshape(128, 256), cq, preferred_element_type=F32)
        send[rows] = pulled.astype(BF).reshape(8, 16, 576)
        return carry

    lax.fori_loop(0, 8, pick, 0)
    keys[si, g] = send[si]
    for (dz, dy, dc) in peers():
        to = sid(z + dz, y + dy, lax.rem(c + dc, 2))
        go(rcopy(send.at[to], keys.at[si, g], as_.at[dz, dy, dc], ar.at[dz, dy, dc], to, g))
    z_step(1, 4)

    qn[...] = jnp.swapaxes(qn_in[...].astype(F32), 0, 1).astype(BF)
    do[...] = jnp.swapaxes(do_in[...].astype(F32), 0, 1).astype(BF)
    qf[:, 512:576] = jnp.swapaxes(qr_in[...].astype(F32), 0, 1).reshape(512, 64).astype(BF)
    chosen = jnp.zeros((16, 64), F32)
    places = lax.broadcasted_iota(jnp.int32, (16, 64), 1)
    picks = sel[...]
    for k in range(32):
        chosen = jnp.where(picks[:, k:k + 1] == places, 1.0, chosen)
    spread = jnp.where(
        lax.rem(lax.broadcasted_iota(jnp.int32, (16, 512), 1), 16) == lax.broadcasted_iota(jnp.int32, (16, 512), 0), 1.0, 0.0
    )
    held = lax.dot_general(chosen.astype(BF), spread.astype(BF), TN, preferred_element_type=F32)
    bias[...] = jnp.where(held > 0.5, 0.0, NEG)

    for t in range(9):
        if t < 8:
            y_near(0, ORDER_W[t])
        if t >= 1:
            y_far(0, ORDER_W[t - 1])
    for t in range(8):
        y_send(1, ORDER_W[t])
    own.wait()

    def x_part(i, who, d=None):
        base = 8 * lax.rem(z + ZN - i, ZN)
        if d is None:
            return keys.at[pl.ds(base, 8), who]
        return keys.at[pl.ds(base + 4 * d, 4), who]

    def x_start(i):
        for dy in range(YN):
            for dc in range(2):
                if (i, dy, dc) != (0, 0, 0):
                    s = sid(z + (ZN - i), y + (YN - dy), lax.rem(c + dc, 2))
                    rcopy(send.at[s], keys.at[s, g], as_.at[i, dy, dc], ar.at[i, dy, dc], s, g).wait_recv()
        ref = x_part(i, g)
        go(rcopy(ref, ref, xs.at[i, 0, 0], xr.at[i, 0, 0], si, gr))
        go(rcopy(ref, ref, xs.at[i, 1, 0], xr.at[i, 1, 0], si, gl))

    def x_fwd(i):
        for d in range(2):
            who, to = (gl, gr) if d == 0 else (gr, gl)
            ref = x_part(i, who)
            rcopy(ref, ref, xs.at[i, d, 0], xr.at[i, d, 0], si, to).wait_recv()
            h = x_part(i, who, d)
            go(rcopy(h, h, xs.at[i, d, 1], xr.at[i, d, 1], si, to))

    def x_done(i):
        for d in range(2):
            h = x_part(i, gf, d)
            rcopy(h, h, xs.at[i, d, 1], xr.at[i, d, 1], si, gr if d == 0 else gl).wait_recv()

    x_start(ORDER[0])
    x_start(ORDER[1])
    x_fwd(ORDER[0])
    sib_wait(0)

    rep = jnp.where(
        lax.broadcasted_iota(jnp.int32, (128, 512), 1) // 4 == lax.broadcasted_iota(jnp.int32, (128, 512), 0), 1.0, 0.0
    ).astype(BF)
    lb_mask = lax.rem(lax.broadcasted_iota(jnp.int32, (64, 512), 1), 4) == (
        lax.broadcasted_iota(jnp.int32, (64, 512), 0) // 16
    )

    def weight(i):
        return wall[:, i].astype(F32).reshape(512, 128).astype(BF)

    def rows16(h):
        return pl.ds(pl.multiple_of(16 * h, 16), 16)

    def project_q(h, carry):
        wide = jnp.dot(qn[h], rep, preferred_element_type=F32)
        wide = jnp.where(lb_mask, jnp.concatenate([wide] * 4, axis=0), 0.0).astype(BF)
        lat = jnp.dot(wide, weight(h), preferred_element_type=F32)
        qf[rows16(h), 0:512] = jnp.concatenate([lat[16 * b:16 * b + 16] for b in range(4)], axis=1).astype(BF)
        return carry

    lax.fori_loop(0, 32, project_q, 0)

    def chunk_keys(zz):
        return keys[pl.ds(8 * zz, 8)].reshape(512, 576)

    def score(i, m, l):
        zz = lax.rem(z + ZN - i, ZN)
        s = lax.dot_general(chunk_keys(zz), qf[...], NT, preferred_element_type=F32) * SCALE
        b = bias[pl.ds(pl.multiple_of(8 * zz, 8), 8), :]
        s = (s.reshape(8, 64, 512) + b[:, None, :]).reshape(512, 512)
        mn = jnp.maximum(m, jnp.max(s, axis=0, keepdims=True))
        e = jnp.exp(s - mn)
        e_ref[zz] = e
        mj_ref[zz] = mn
        return mn, l * jnp.exp(m - mn) + jnp.sum(e, axis=0, keepdims=True)

    zero = jnp.zeros((1, 512), F32)
    m, l = zero + NEG, zero
    for t in range(8):
        y_near(1, ORDER_W[t])
        if t >= 1:
            y_far(1, ORDER_W[t - 1])
        if t < 6:
            x_start(ORDER[t + 2])
        if t < 7:
            x_fwd(ORDER[t + 1])
        x_done(ORDER[t])
        m, l = lax.fori_loop(t, t + 1, lambda k, ml: score(step_of(k), *ml), (m, l))
    y_far(1, ORDER_W[7])
    sib_wait(1)
    inv = 1.0 / l

    def project_d(h, carry):
        dol[rows16(h), :] = lax.dot_general(do[h], weight(32 + h), NT, preferred_element_type=F32).astype(BF)
        return carry

    lax.fori_loop(0, 32, project_d, 0)

    def back(j, d):
        p = e_ref[j] * (jnp.exp(mj_ref[j] - m) * inv)
        dp = lax.dot_general(keys[pl.ds(8 * j, 8)].reshape(512, 576)[:, :512], dol[...], NT, preferred_element_type=F32)
        e_ref[j] = p
        dp_ref[j] = dp
        return d + jnp.sum(p * dp, axis=0, keepdims=True)

    delta = lax.fori_loop(0, 8, back, zero)
    dqt[...] = jnp.zeros_like(dqt)
    ot[...] = jnp.zeros_like(ot)

    def grads(t, carry):
        zz = lax.rem(z + step_of(t + 4), ZN)
        kj = chunk_keys(zz)
        p = e_ref[zz]
        pb = p.astype(BF)
        ds = (p * (dp_ref[zz] - delta) * SCALE).astype(BF)
        gk = jnp.dot(ds, qf[...], preferred_element_type=F32)
        gv = jnp.dot(pb, dol[...], preferred_element_type=F32)
        gk = jnp.concatenate([gk[:, :512] + gv, gk[:, 512:]], axis=1)
        dk[pl.ds(8 * zz, 8)] = gk.astype(BF).reshape(8, 4, 16, 576)
        dqt[...] += lax.dot_general(kj, ds, TN, preferred_element_type=F32)
        ot[...] += lax.dot_general(kj[:, :512], pb, TN, preferred_element_type=F32)
        return carry

    def lo(i):
        return pl.ds(8 * lax.rem(z + i, ZN), 4)

    def hi(i):
        return pl.ds(8 * lax.rem(z + i, ZN) + 4, 4)

    def leave(i):
        go(rcopy(dk.at[lo(i), gf], fl.at[i], fs.at[i, 0], fq.at[i, 0], si, gr))
        go(rcopy(dk.at[hi(i), gf], fr.at[i], fs.at[i, 1], fq.at[i, 1], si, gl))
        go(rcopy(dk.at[hi(i), gr], nl.at[hi(i)], ns.at[i, 0, 0], nq.at[i, 0, 0], si, gr))
        go(rcopy(dk.at[lo(i), gl], nr.at[lo(i)], ns.at[i, 1, 0], nq.at[i, 1, 0], si, gl))

    def combine(i):
        rcopy(fl.at[i], fl.at[i], fs.at[i, 0], fq.at[i, 0], si, gr).wait_recv()
        tor[i] = (dk[lo(i), gr].astype(F32) + fl[i].astype(F32)).astype(BF)
        rcopy(fr.at[i], fr.at[i], fs.at[i, 1], fq.at[i, 1], si, gl).wait_recv()
        tol[i] = (dk[hi(i), gl].astype(F32) + fr[i].astype(F32)).astype(BF)
        go(rcopy(tor.at[i], nl.at[lo(i)], ns.at[i, 0, 1], nq.at[i, 0, 1], si, gr))
        go(rcopy(tol.at[i], nr.at[hi(i)], ns.at[i, 1, 1], nq.at[i, 1, 1], si, gl))

    def owner(i):
        rcopy(nl.at[hi(i)], nl.at[hi(i)], ns.at[i, 0, 0], nq.at[i, 0, 0], si, gr).wait_recv()
        rcopy(nr.at[lo(i)], nr.at[lo(i)], ns.at[i, 1, 0], nq.at[i, 1, 0], si, gl).wait_recv()
        rcopy(nl.at[lo(i)], nl.at[lo(i)], ns.at[i, 0, 1], nq.at[i, 0, 1], si, gr).wait_recv()
        rcopy(nr.at[hi(i)], nr.at[hi(i)], ns.at[i, 1, 1], nq.at[i, 1, 1], si, gl).wait_recv()
        al = pl.ds(8 * lax.rem(z + i, ZN), 8)
        back_send[al] = (dk[al, g].astype(F32) + nl[al].astype(F32) + nr[al].astype(F32)).astype(BF)
        for dy in range(YN):
            for dc in range(2):
                if (i, dy, dc) != (0, 0, 0):
                    to = sid(z + i, y + dy, lax.rem(c + dc, 2))
                    go(rcopy(back_send.at[to], got.at[si], bs.at[i, dy, dc], br.at[i, dy, dc], to, g))

    back_send = at_t
    rorder = [(5 * (t + 4)) % 8 for t in range(8)]
    for t in range(8):
        lax.fori_loop(t, t + 1, grads, 0)
        leave(rorder[t])
        if t >= 2:
            combine(rorder[t - 2])
        if t >= 4:
            owner(rorder[t - 4])
    combine(rorder[6])
    owner(rorder[4])
    ol[...] = jnp.transpose(ot[...]).astype(BF)
    dql[...] = jnp.transpose(dqt[0:512, :]).astype(BF)
    dqr[...] = jnp.swapaxes(jnp.transpose(dqt[512:576, :]).reshape(32, 16, 64), 0, 1).astype(BF)
    combine(rorder[7])
    owner(rorder[5])

    def finish(h, carry):
        qn[h] = jnp.dot(ol[rows16(h), :], weight(32 + h), preferred_element_type=F32).astype(BF)
        x = dql[rows16(h), :]
        x = jnp.concatenate([x[:, 128 * b:128 * b + 128] for b in range(4)], axis=0)
        r = lax.dot_general(x, weight(h), NT, preferred_element_type=F32)
        r = jnp.where(lb_mask, r, 0.0)
        ot[rows16(h), :] = r[0:16] + r[16:32] + r[32:48] + r[48:64]
        return carry

    lax.fori_loop(0, 16, finish, 0)
    owner(rorder[6])
    lax.fori_loop(16, 32, finish, 0)
    owner(rorder[7])
    attn[...] = jnp.swapaxes(qn[...].astype(F32), 0, 1).astype(BF)
    gv0 = ot[...]
    g0 = gv0.astype(BF)
    r1 = gv0 - g0.astype(F32)
    g1 = r1.astype(BF)
    g2 = (r1 - g1.astype(F32)).astype(BF)
    acc = lax.dot_general(g0, rep, NT, preferred_element_type=F32)
    acc += lax.dot_general(g1, rep, NT, preferred_element_type=F32)
    acc += lax.dot_general(g2, rep, NT, preferred_element_type=F32)
    dqn[...] = jnp.swapaxes(acc.reshape(32, 16, 128), 0, 1).astype(BF)

    got[si] = back_send[si]
    for i in rorder:
        for dy in range(YN):
            for dc in range(2):
                if (i, dy, dc) != (0, 0, 0):
                    s = sid(z + (ZN - i), y + (YN - dy), lax.rem(c + dc, 2))
                    rcopy(got.at[s], got.at[s], bs.at[i, dy, dc], br.at[i, dy, dc], s, g).wait_recv()
    total = lax.dot_general(m_ref[...].reshape(1024, 256), got[...].reshape(1024, 576), TN, preferred_element_type=F32)
    out[:, g] = total.astype(BF).reshape(16, 16, 576)
    ref = out.at[:, g]
    go(rcopy(ref, ref, gs.at[0, 0], gq.at[0, 0], si, gr))
    go(rcopy(ref, ref, gs.at[1, 0], gq.at[1, 0], si, gl))
    for d in range(2):
        who, to = (gl, gr) if d == 0 else (gr, gl)
        ref = out.at[:, who]
        rcopy(ref, ref, gs.at[d, 0], gq.at[d, 0], si, to).wait_recv()
        h = out.at[pl.ds(8 * d, 8), who]
        go(rcopy(h, h, gs.at[d, 1], gq.at[d, 1], si, to))
    for d in range(2):
        h = out.at[pl.ds(8 * d, 8), gf]
        rcopy(h, h, gs.at[d, 1], gq.at[d, 1], si, gr if d == 0 else gl).wait_recv()
    for cp in late:
        cp.wait_send()


def vm():
    return pl.BlockSpec(memory_space=pltpu.VMEM)


def whole(*args):
    dma = pltpu.SemaphoreType.DMA
    v = pltpu.VMEM
    half = v((8, 4, 16, 576), BF)
    quarter = v((64, 16, 576), BF)
    return pl.pallas_call(
        whole_kernel,
        name="whole",
        out_shape=(
            jax.ShapeDtypeStruct((16, 32, 128), BF),
            jax.ShapeDtypeStruct((16, 32, 128), BF),
            jax.ShapeDtypeStruct((16, 32, 64), BF),
            jax.ShapeDtypeStruct((16, 4, 16, 576), BF),
        ),
        in_specs=[vm()] * 8,
        out_specs=(vm(),) * 4,
        scratch_shapes=[
            v((64, 8, 128), BF), v((64, 64, 8, 128), BF), v((64, 1, 64), jnp.int32), v((64, 16, 256), BF), quarter,
            v((64, 4, 16, 576), BF),
            v((32, 16, 128), BF), v((32, 16, 128), BF), v((512, 576), BF), v((512, 512), BF), v((64, 512), F32),
            v((8, 512, 512), F32), v((8, 512, 512), F32), v((8, 1, 512), F32), v((64, 4, 16, 576), BF),
            v((576, 512), F32), v((512, 512), F32), v((512, 512), BF), v((512, 512), BF),
            quarter, half, half, quarter, quarter, half, half, quarter,
            dma((2, 2, 4)), dma((2, 2, 4)),
            dma((2, 8, 2, 2)), dma((2, 8, 2, 2)),
            dma((2, 8, 4)), dma((2, 8, 4)),
            dma((8, 4, 2)), dma((8, 4, 2)),
            dma((8, 4, 2)), dma((8, 4, 2)),
            dma((8, 2, 2)), dma((8, 2, 2)),
            dma((2,)),
            dma((8, 2)), dma((8, 2)),
            dma((8, 2, 2)), dma((8, 2, 2)),
            dma((8, 4, 2)), dma((8, 4, 2)),
            dma((2, 2)), dma((2, 2)),
        ],
        compiler_params=pltpu.CompilerParams(has_side_effects=True, collective_id=0, vmem_limit_bytes=67043328),
    )(*args)


def local(q_nope, q_rope, cache, w_uk, w_uv, d_out, sel, slot_blocks):
    attn, dqn, dqr, dc = whole(
        q_nope, q_rope, d_out, cache.reshape(16, 4, 16, 576), w_uk, w_uv, sel, slot_blocks
    )
    return (attn, dqn, dqr, dc.astype(F32).reshape(1024, 576))

def solution(mesh):
    return jax.shard_map(
        local,
        mesh=mesh,
        in_specs=(
            P("seq", "grp", None),
            P("seq", "grp", None),
            P("seq", None),
            P("grp", "seq"),
            P("grp", "seq"),
            P("seq", "grp", None),
            P("seq", None),
            P("seq", None),
        ),
        out_specs=(
            P("seq", "grp", None),
            P("seq", "grp", None),
            P("seq", "grp", None),
            P("seq", None),
        ),
        check_vma=False,
    )
```

time: 529 us -> 206 us (0.39)
  waiting for transfers between devices: 283 us -> 0 us
  Pallas kernels: 0 us -> 197 us
  matrix products: 84 us -> 0 us
  local copies, waits for them, and re-layouts: 83.7 us -> 6.38 us
  other arithmetic: 32.5 us -> 1.49 us
  starting transfers between devices: 26.4 us -> 0 us
  between operations: 14.1 us -> 0.67 us
    pallas_call x0 -> x1, Pallas kernels: none -> 197 us  [whole(): pl.pallas_call(whole_kernel, name='whole', out_shape=(jax.ShapeDtypeStruc...]
    all_gather x2 -> x0, waiting for transfers between devices: 148 us -> none  [the longest x1 80.6 us: local(): lax.all_gather(w_uk, 'seq', axis=1, tiled=True)]
    all_to_all x3 -> x0, waiting for transfers between devices: 106 us -> none  [the longest x1 98.3 us: local(): lax.all_to_all(dkeys.reshape(peers, per_peer, BLOCK_LEN * width).astype(j...]
    dot_general x10 -> x0, matrix products: 73.3 us -> none  [the longest x1 18.8 us: local(): jnp.einsum('qht,qhc->tc', dscore, qfull, preferred_element_type=jnp.float32)]
    unnamed x25 -> x11, local copies, waits for them, and re-layouts: 45.4 us -> 6.38 us
    convert_element_type x1 -> x0, other arithmetic: 29.9 us -> none  [local(): dkeys.reshape(peers, per_peer, BLOCK_LEN * width).astype(jnp.bfloat16)]
    convert_element_type x3 -> x0, local copies, waits for them, and re-layouts: 29.9 us -> none  [local(): dkeys.reshape(peers, per_peer, BLOCK_LEN * width).astype(jnp.bfloat16)]
    psum x1 -> x0, waiting for transfers between devices: 28.2 us -> none  [local(): lax.psum(local_grad.astype(jnp.bfloat16), 'grp').astype(jnp.float32)]
  transfers between devices with their start and end apart: 6 -> 0, of which waited for: 5 -> 0; matrix products, arithmetic and copies ran while one was open for 9% -> 0% of each run, Pallas kernels for 0% -> 0%
where the time goes in v2:
time: 206 us; the launch traced here: 205 us
  Pallas kernels  197 us (96%)
  local copies, waits for them, and re-layouts  6.38 us (3%)
    pallas_call x1, Pallas kernels, whole(): pl.pallas_call(whole_kernel, name='whole', out_shape=(jax.ShapeDtypeStruc...  197 us
    unnamed x11, local copies, waits for them, and re-layouts  6.38 us

profile of v2, /device:TPU:1, one launch (start us, length us, event | category | flops | bytes accessed | tf_op | source)
XLA Modules:
  0.0 205.0 jit_solution(4344264123204395942)
XLA Ops:
  0.6 2.4 %copy.12 = bf16[1024,576]{1,0:T(8,128)(2,1)} copy(bf16[1024,576]{0,1:T(8,128)(2,1)} %param.10) | data formatting | bytes 2359296 | tf_op args[2]
  3.0 196.5 %whole.1 = (bf16[16,32,128]{2,1,0:T(8,128)(2,1)}, bf16[16,32,128]{2,1,0:T(8,128)(2,1)}, bf16[16,32,64]{2,1,0:T(8,128)(2,1)}, bf16[16,4,16,576]{3,2,1,0:T(8,128)(2,1)}) custom-call(bf16[16,32,128]{2,1,0:T(8,128)(2,1)} %qn_in.1, bf16[16,32,64]{2,1,0:T(8,128)(2,1)} %qr_in.1, bf16[16,32,128]{2,1,0:T(8,128)(2,1)} %do_in.1, bf16[16,4,16,576]{3,2,1,0:T(8,128)(2,1)} %bitcast.4, ...), custom_call_target="tpu_custom_call" | custom-call | tf_op jit(solution)/shard_map/whole/pallas_call | solution.py:441
  199.5 1.5 bitcast_convert_fusion
  201.0 0.0 copy-start.2
  201.0 0.0 copy-start.1
  201.1 0.0 copy-start
  201.1 2.0 copy.13
  203.1 0.0 copy-done.2
  203.1 0.7 copy.17
  203.7 0.0 copy-done.1
  203.7 0.7 copy.18
  204.4 0.0 copy-done
  204.4 0.7 copy.19
Async XLA Ops:
  201.0 2.0 copy-start.2
  201.0 2.7 %copy-start.1 = (bf16[16,32,128]{2,1,0:T(8,128)(2,1)S(1)}, bf16[16,32,128]{2,1,0:T(8,128)(2,1)}, u32[]{:S(2)}) copy-start(bf16[16,32,128]{2,1,0:T(8,128)(2,1)} %get-tuple-element.21) | copy-start | bytes 393220
  201.1 3.3 %copy-start = (bf16[16,32,64]{2,1,0:T(8,128)(2,1)S(1)}, bf16[16,32,64]{2,1,0:T(8,128)(2,1)}, u32[]{:S(2)}) copy-start(bf16[16,32,64]{2,1,0:T(8,128)(2,1)} %get-tuple-element.22) | copy-start | bytes 196612

commit v3 on v2

v3 whole, which is shorter than its diff:
```python
import math

import jax
import jax.numpy as jnp
from jax import lax
from jax.experimental import pallas as pl
from jax.experimental.pallas import tpu as pltpu
from jax.sharding import PartitionSpec as P

MESH = pl.DeviceIdType.MESH
BF = jnp.bfloat16
F32 = jnp.float32
ZN, YN, XN = 8, 4, 4
ORDER = (0, 1, 7, 2, 6, 3, 5, 4)
RORDER = (4, 3, 5, 2, 6, 1, 7, 0)
NEG = -1e30


def rcopy(src, dst, ssem, rsem, seq, grp):
    return pltpu.make_async_remote_copy(
        src_ref=src, dst_ref=dst, send_sem=ssem, recv_sem=rsem,
        device_id=(seq, grp), device_id_type=MESH,
    )


def place():
    si = lax.axis_index("seq")
    g = lax.axis_index("grp")
    c = lax.rem(si, 2)
    y = lax.rem(si // 2, YN)
    z = si // (2 * YN)
    return si, g, z, y, c


def sid(z, y, c):
    return (lax.rem(z, ZN) * YN + lax.rem(y, YN)) * 2 + c


def peers():
    return [(dz, dy, dc) for dz in ORDER for dy in range(YN) for dc in range(2) if (dz, dy, dc) != (0, 0, 0)]


NT = (((1,), (1,)), ((), ()))
TN = (((0,), (0,)), ((), ()))
SCALE = 1.0 / math.sqrt(192.0)


def whole_kernel(qn_in, qr_in, do_in, cache, wk_in, wv_in, sel, slot,
                 attn, dqn, dqr, out,
                 wsh, wall, table, m_ref, send, keys,
                 qn, do, qf, dol, bias, e_ref, dp_ref, mj_ref, dk,
                 dqt, ot, ol, dql, at_t, fl, fr, nl, nr, tol, tor, got,
                 sent, zr, yr, yq, sr, ixr, ar, xr, xq, fq, nq, br, gr_, gq, loc):
    si, g, z, y, c = place()
    zp, zm = sid(z + 1, y, c), sid(z + 7, y, c)
    yp, ym = sid(z, y + 1, c), sid(z, y + 3, c)
    sib = sid(z, y, 1 - c)
    gr, gl, gf = lax.rem(g + 1, XN), lax.rem(g + 3, XN), lax.rem(g + 2, XN)
    barrier = pltpu.get_barrier_semaphore()
    for (dz, dy, dc) in peers():
        pl.semaphore_signal(barrier, inc=1, device_id=(sid(z + dz, y + dy, lax.rem(c + dc, 2)), g), device_id_type=MESH)
    pl.semaphore_signal(barrier, inc=1, device_id=(si, gr), device_id_type=MESH)
    pl.semaphore_signal(barrier, inc=1, device_id=(si, gl), device_id_type=MESH)

    for i, w_in in ((0, wk_in), (32, wv_in)):
        wsh[i:i + 32] = w_in[...].astype(F32).reshape(32, 8, 128).astype(BF)
    pl.semaphore_wait(barrier, 65)

    def go(src, dst, kind, rsem, seq, grp):
        rcopy(src, dst, sent.at[kind], rsem, seq, grp).start()

    def here(ref, rsem):
        rcopy(ref, ref, sent.at[0], rsem, sib, g).wait_recv()

    def gone(ref, kind):
        rcopy(ref, ref, sent.at[kind], loc.at[0], sib, g).wait_send()

    def src_of(a, b):
        return sid(z + (ZN - a), y + (YN - b), c)

    def tiles(ref, kv, h=None):
        if h is None:
            return ref.at[pl.ds(32 * kv, 32)]
        return ref.at[pl.ds(32 * kv + 16 * h, 16)]

    own = pltpu.make_async_copy(wsh, wall.at[si], loc.at[0])
    mine = pltpu.make_async_copy(slot, table.at[si], loc.at[1])
    mine.start()
    for (dz, dy, dc) in peers():
        to = sid(z + dz, y + dy, lax.rem(c + dc, 2))
        go(slot, table.at[si], 1, ixr.at[0], to, g)
    for kv in range(2):
        go(tiles(wsh, kv), tiles(wall.at[si], kv), 0, zr.at[kv, 0, 0], zp, g)
        go(tiles(wsh, kv), tiles(wall.at[si], kv), 0, zr.at[kv, 1, 0], zm, g)
    own.start()

    def y_send(kv, a):
        s = src_of(a, 0)
        ref = tiles(wsh if a == 0 else wall.at[s], kv)
        dst = tiles(wall.at[s], kv)
        go(ref, dst, 0, yr.at[kv, a, 0], yp, g)
        go(ref, dst, 0, yr.at[kv, a, 1], ym, g)
        go(ref, dst, 0, sr.at[kv], sib, g)

    def z_step(kv, k):
        for d in range(2):
            a = k if d == 0 else ZN - k
            s = src_of(a, 0)
            here(tiles(wall.at[s], kv) if k < 4 else tiles(wall.at[s], kv, d), zr.at[kv, d, k - 1])
            if k < 4:
                nxt = tiles(wall.at[s], kv) if k < 3 else tiles(wall.at[s], kv, d)
                go(nxt, nxt, 0, zr.at[kv, d, k], zp if d == 0 else zm, g)

    def y_near(kv, a):
        for d in range(2):
            ref = wall.at[src_of(a, 1 if d == 0 else 3)]
            here(tiles(ref, kv), yr.at[kv, a, d])
            go(tiles(ref, kv, d), tiles(ref, kv, d), 0, yq.at[kv, a], yp if d == 0 else ym, g)
            go(tiles(ref, kv), tiles(ref, kv), 0, sr.at[kv], sib, g)

    def y_far(kv, a):
        ref = tiles(wall.at[src_of(a, 2)], kv)
        here(ref, yq.at[kv, a])
        go(ref, ref, 0, sr.at[kv], sib, g)

    def sib_wait(kv):
        here(wall.at[pl.ds(0, 16)], sr.at[kv])

    y_send(0, 0)
    rep = jnp.where(
        lax.broadcasted_iota(jnp.int32, (128, 512), 1) // 4 == lax.broadcasted_iota(jnp.int32, (128, 512), 0), 1.0, 0.0
    ).astype(BF)
    qn[...] = jnp.swapaxes(qn_in[...].astype(F32), 0, 1).astype(BF)
    ol[...] = jnp.dot(qn[...].reshape(512, 128), rep, preferred_element_type=F32).astype(BF)
    z_step(0, 1)
    y_send(0, 1)
    y_send(0, 7)
    mine.wait()
    here(table.at[pl.ds(0, 63)], ixr.at[0])

    lane = lax.broadcasted_iota(jnp.int32, (1, 64), 1)
    col = lax.broadcasted_iota(jnp.int32, (16, 256), 1)
    row = lax.broadcasted_iota(jnp.int32, (16, 256), 0)
    colb, same = col // 16, lax.rem(col, 16) == row

    def build(i, carry):
        for k in range(8):
            r = 8 * i + k
            v = jnp.sum(jnp.where(lane == si, table[r].astype(F32), 0.0), axis=1, keepdims=True).astype(jnp.int32)
            hit = (colb == jnp.broadcast_to(v, (16, 256))) & same
            m_ref[r] = jnp.where(hit, 1.0, 0.0).astype(BF)
        return carry

    lax.fori_loop(0, 8, build, 0)
    cq = cache[:, g].reshape(256, 576)

    def pick(i, carry):
        rows = pl.ds(8 * i, 8)
        pulled = jnp.dot(m_ref[rows].reshape(128, 256), cq, preferred_element_type=F32)
        send[rows] = pulled.astype(BF).reshape(8, 16, 576)
        return carry

    lax.fori_loop(0, 8, pick, 0)
    keys[si, g] = send[si]

    def ask(t):
        i = ORDER[t]
        for dy in range(YN):
            for dc in range(2):
                if (i, dy, dc) != (0, 0, 0):
                    to = sid(z + i, y + dy, lax.rem(c + dc, 2))
                    go(send.at[to], keys.at[si, g], 2, ar.at[i], to, g)

    ask(0)
    z_step(0, 2)
    y_send(0, 2)
    y_send(0, 6)
    z_step(1, 1)
    y_near(0, 0)
    z_step(0, 3)
    y_send(0, 3)
    y_send(0, 5)
    z_step(1, 2)
    ask(1)
    ask(2)
    y_near(0, 1)
    z_step(0, 4)
    y_send(0, 4)
    z_step(1, 3)
    z_step(1, 4)
    ask(3)
    ask(4)
    ask(5)
    ask(6)
    ask(7)
    own.wait()

    do[...] = jnp.swapaxes(do_in[...].astype(F32), 0, 1).astype(BF)
    qf[:, 512:576] = jnp.swapaxes(qr_in[...].astype(F32), 0, 1).reshape(512, 64).astype(BF)
    chosen = jnp.zeros((16, 64), F32)
    places = lax.broadcasted_iota(jnp.int32, (16, 64), 1)
    picks = sel[...]
    for k in range(32):
        chosen = jnp.where(picks[:, k:k + 1] == places, 1.0, chosen)
    spread = jnp.where(
        lax.rem(lax.broadcasted_iota(jnp.int32, (16, 512), 1), 16) == lax.broadcasted_iota(jnp.int32, (16, 512), 0), 1.0, 0.0
    )
    held = lax.dot_general(chosen.astype(BF), spread.astype(BF), TN, preferred_element_type=F32)
    bias[...] = jnp.where(held > 0.5, 0.0, NEG)

    def x_part(i, who, d=None):
        base = 8 * lax.rem(z + ZN - i, ZN)
        if d is None:
            return keys.at[pl.ds(base, 8), who]
        return keys.at[pl.ds(base + 4 * d, 4), who]

    def x_start(i):
        ref = x_part(i, g)
        here(keys.at[pl.ds(0, 7), g] if i == 0 else ref, ar.at[i])
        go(ref, ref, 3, xr.at[i, 0], si, gr)
        go(ref, ref, 3, xr.at[i, 1], si, gl)

    def x_fwd(i):
        for d in range(2):
            who, to = (gl, gr) if d == 0 else (gr, gl)
            here(x_part(i, who), xr.at[i, d])
            go(x_part(i, who, d), x_part(i, who, d), 3, xq.at[i], si, to)

    def x_done(i):
        here(x_part(i, gf), xq.at[i])

    lb_mask = lax.rem(lax.broadcasted_iota(jnp.int32, (64, 512), 1), 4) == (
        lax.broadcasted_iota(jnp.int32, (64, 512), 0) // 16
    )

    def weight(i):
        return wall[:, i].astype(F32).reshape(512, 128).astype(BF)

    def rows16(h):
        return pl.ds(pl.multiple_of(16 * h, 16), 16)

    def project_q(h, carry):
        wide = jnp.where(lb_mask, jnp.concatenate([ol[rows16(h), :].astype(F32)] * 4, axis=0), 0.0).astype(BF)
        lat = jnp.dot(wide, weight(h), preferred_element_type=F32)
        qf[rows16(h), 0:512] = jnp.concatenate([lat[16 * b:16 * b + 16] for b in range(4)], axis=1).astype(BF)
        return carry

    def project_d(h, carry):
        dol[rows16(h), :] = lax.dot_general(do[h], weight(32 + h), NT, preferred_element_type=F32).astype(BF)
        return carry

    def chunk_keys(zz):
        return keys[pl.ds(8 * zz, 8)].reshape(512, 576)

    def score(i, m, l):
        zz = lax.rem(z + ZN - i, ZN)
        s = lax.dot_general(chunk_keys(zz), qf[...], NT, preferred_element_type=F32) * SCALE
        b = bias[pl.ds(pl.multiple_of(8 * zz, 8), 8), :]
        s = (s.reshape(8, 64, 512) + b[:, None, :]).reshape(512, 512)
        mn = jnp.maximum(m, jnp.max(s, axis=0, keepdims=True))
        e = jnp.exp(s - mn)
        e_ref[zz] = e
        mj_ref[zz] = mn
        return mn, l * jnp.exp(m - mn) + jnp.sum(e, axis=0, keepdims=True)

    zero = jnp.zeros((1, 512), F32)
    state = [zero + NEG, zero]

    def yn(kv, t):
        y_near(kv, ORDER[t])

    def yf(kv, t):
        y_far(kv, ORDER[t])

    def ys1(t):
        y_send(1, ORDER[t])

    def sc(t):
        x_done(ORDER[t])
        state[:] = score(ORDER[t], *state)

    def pq(h):
        lax.fori_loop(h, h + 8, project_q, 0, unroll=2)

    def pd(h):
        lax.fori_loop(h, h + 8, project_d, 0, unroll=2)

    def xst(t):
        x_start(ORDER[t])

    def xf(t):
        x_fwd(ORDER[t])

    xst(0)
    yf(0, 0)
    yn(0, 2)
    xf(0)
    xst(1)
    yf(0, 1)
    yn(0, 3)
    xst(2)
    xf(1)
    yn(0, 4)
    yf(0, 2)
    xf(2)
    yn(0, 5)
    yf(0, 3)
    yn(0, 6)
    yf(0, 4)
    xst(3)
    yn(0, 7)
    yf(0, 5)
    ys1(0)
    ys1(1)
    ys1(2)
    ys1(3)
    ys1(4)
    ys1(5)
    ys1(6)
    ys1(7)
    xst(4)
    xf(3)
    yf(0, 6)
    yf(0, 7)
    xf(4)
    sib_wait(0)
    pq(0)
    pq(8)
    yn(1, 0)
    pq(16)
    pq(24)
    sc(0)
    sc(1)
    yn(1, 1)
    yf(1, 0)
    sc(2)
    xst(5)
    yn(1, 2)
    yf(1, 1)
    sc(3)
    xst(6)
    xf(5)
    yn(1, 3)
    yf(1, 2)
    sc(4)
    xf(6)
    yn(1, 4)
    yf(1, 3)
    xst(7)
    yn(1, 5)
    yf(1, 4)
    sc(5)
    yn(1, 6)
    yf(1, 5)
    sc(6)
    yn(1, 7)
    xf(7)
    yf(1, 6)
    yf(1, 7)
    sib_wait(1)
    pd(0)
    pd(8)
    pd(16)
    pd(24)
    sc(7)
    m, l = state
    inv = 1.0 / l

    def back(j, d):
        p = e_ref[j] * (jnp.exp(mj_ref[j] - m) * inv)
        dp = lax.dot_general(keys[pl.ds(8 * j, 8)].reshape(512, 576)[:, :512], dol[...], NT, preferred_element_type=F32)
        e_ref[j] = p
        dp_ref[j] = dp
        return d + jnp.sum(p * dp, axis=0, keepdims=True)

    delta = lax.fori_loop(0, 8, back, zero)
    dqt[...] = jnp.zeros_like(dqt)
    ot[...] = jnp.zeros_like(ot)

    def grads(i):
        zz = lax.rem(z + i, ZN)
        kj = chunk_keys(zz)
        p = e_ref[zz]
        pb = p.astype(BF)
        ds = (p * (dp_ref[zz] - delta) * SCALE).astype(BF)
        gk = jnp.dot(ds, qf[...], preferred_element_type=F32)
        gv = jnp.dot(pb, dol[...], preferred_element_type=F32)
        gk = jnp.concatenate([gk[:, :512] + gv, gk[:, 512:]], axis=1)
        dk[pl.ds(8 * zz, 8)] = gk.astype(BF).reshape(8, 4, 16, 576)
        dqt[...] += lax.dot_general(kj, ds, TN, preferred_element_type=F32)
        ot[...] += lax.dot_general(kj[:, :512], pb, TN, preferred_element_type=F32)

    def lo(i):
        return pl.ds(8 * lax.rem(z + i, ZN), 4)

    def hi(i):
        return pl.ds(8 * lax.rem(z + i, ZN) + 4, 4)

    def leave(i):
        go(dk.at[lo(i), gf], fl.at[i], 4, fq.at[i, 0], si, gr)
        go(dk.at[hi(i), gf], fr.at[i], 4, fq.at[i, 1], si, gl)
        go(dk.at[hi(i), gr], nl.at[hi(i)], 4, nq.at[i], si, gr)
        go(dk.at[lo(i), gl], nr.at[lo(i)], 4, nq.at[i], si, gl)

    def combine(i):
        here(fl.at[i], fq.at[i, 0])
        tor[i] = (dk[lo(i), gr].astype(F32) + fl[i].astype(F32)).astype(BF)
        here(fr.at[i], fq.at[i, 1])
        tol[i] = (dk[hi(i), gl].astype(F32) + fr[i].astype(F32)).astype(BF)
        go(tor.at[i], nl.at[lo(i)], 4, nq.at[i], si, gr)
        go(tol.at[i], nr.at[hi(i)], 4, nq.at[i], si, gl)

    def owner(i):
        here(dk.at[pl.ds(0, 4)], nq.at[i])
        al = pl.ds(8 * lax.rem(z + i, ZN), 8)
        back_send[al] = (dk[al, g].astype(F32) + nl[al].astype(F32) + nr[al].astype(F32)).astype(BF)
        for dy in range(YN):
            for dc in range(2):
                if (i, dy, dc) != (0, 0, 0):
                    to = sid(z + i, y + dy, lax.rem(c + dc, 2))
                    go(back_send.at[to], got.at[si], 5, br.at[0], to, g)

    back_send = at_t
    for t in range(8):
        grads(RORDER[t])
        leave(RORDER[t])
        if t >= 2:
            combine(RORDER[t - 2])
        if t >= 4:
            owner(RORDER[t - 4])
    combine(RORDER[6])
    owner(RORDER[4])
    gone(wall.at[pl.ds(0, 63)], 0)
    gone(table.at[pl.ds(0, 63)], 1)
    gone(send.at[pl.ds(0, 63)], 2)
    gone(keys.at[pl.ds(0, 48)], 3)
    ol[...] = jnp.transpose(ot[...]).astype(BF)
    combine(RORDER[7])
    owner(RORDER[5])
    dql[...] = jnp.transpose(dqt[0:512, :]).astype(BF)
    owner(RORDER[6])
    dqr[...] = jnp.swapaxes(jnp.transpose(dqt[512:576, :]).reshape(32, 16, 64), 0, 1).astype(BF)
    owner(RORDER[7])
    got[si] = back_send[si]

    def finish(h, carry):
        qn[h] = jnp.dot(ol[rows16(h), :], weight(32 + h), preferred_element_type=F32).astype(BF)
        x = dql[rows16(h), :]
        x = jnp.concatenate([x[:, 128 * b:128 * b + 128] for b in range(4)], axis=0)
        r = lax.dot_general(x, weight(h), NT, preferred_element_type=F32)
        r = jnp.where(lb_mask, r, 0.0)
        ot[rows16(h), :] = r[0:16] + r[16:32] + r[32:48] + r[48:64]
        return carry

    lax.fori_loop(0, 32, finish, 0, unroll=2)
    here(got.at[pl.ds(0, 63)], br.at[0])
    total = lax.dot_general(m_ref[...].reshape(1024, 256), got[...].reshape(1024, 576), TN, preferred_element_type=F32)
    out[:, g] = total.astype(BF).reshape(16, 16, 576)
    ref = out.at[:, g]
    go(ref, ref, 6, gr_.at[0], si, gr)
    go(ref, ref, 6, gr_.at[1], si, gl)
    gone(dk.at[pl.ds(0, 48)], 4)
    gone(back_send.at[pl.ds(0, 63)], 5)
    attn[...] = jnp.swapaxes(qn[...].astype(F32), 0, 1).astype(BF)
    gv0 = ot[...]
    g0 = gv0.astype(BF)
    r1 = gv0 - g0.astype(F32)
    g1 = r1.astype(BF)
    g2 = (r1 - g1.astype(F32)).astype(BF)
    acc = lax.dot_general(g0, rep, NT, preferred_element_type=F32)
    acc += lax.dot_general(g1, rep, NT, preferred_element_type=F32)
    acc += lax.dot_general(g2, rep, NT, preferred_element_type=F32)
    dqn[...] = jnp.swapaxes(acc.reshape(32, 16, 128), 0, 1).astype(BF)
    for d in range(2):
        who, to = (gl, gr) if d == 0 else (gr, gl)
        here(out.at[:, who], gr_.at[d])
        h = out.at[pl.ds(8 * d, 8), who]
        go(h, h, 6, gq.at[0], si, to)
    here(out.at[:, gf], gq.at[0])
    gone(out.at[pl.ds(0, 12)], 6)


def vm():
    return pl.BlockSpec(memory_space=pltpu.VMEM)


def whole(*args):
    dma = pltpu.SemaphoreType.DMA
    v = pltpu.VMEM
    half = v((8, 4, 16, 576), BF)
    quarter = v((64, 16, 576), BF)
    return pl.pallas_call(
        whole_kernel,
        name="whole",
        out_shape=(
            jax.ShapeDtypeStruct((16, 32, 128), BF),
            jax.ShapeDtypeStruct((16, 32, 128), BF),
            jax.ShapeDtypeStruct((16, 32, 64), BF),
            jax.ShapeDtypeStruct((16, 4, 16, 576), BF),
        ),
        in_specs=[vm()] * 8,
        out_specs=(vm(),) * 4,
        scratch_shapes=[
            v((64, 8, 128), BF), v((64, 64, 8, 128), BF), v((64, 1, 64), jnp.int32), v((64, 16, 256), BF), quarter,
            v((64, 4, 16, 576), BF),
            v((32, 16, 128), BF), v((32, 16, 128), BF), v((512, 576), BF), v((512, 512), BF), v((64, 512), F32),
            v((8, 512, 512), F32), v((8, 512, 512), F32), v((8, 1, 512), F32), v((64, 4, 16, 576), BF),
            v((576, 512), F32), v((512, 512), F32), v((512, 512), BF), v((512, 512), BF),
            quarter, half, half, quarter, quarter, half, half, quarter,
            dma((7,)), dma((2, 2, 4)), dma((2, 8, 2)), dma((2, 8)), dma((2,)), dma((1,)), dma((8,)),
            dma((8, 2)), dma((8,)), dma((8, 2)), dma((8,)), dma((1,)), dma((2,)), dma((1,)), dma((2,)),
        ],
        compiler_params=pltpu.CompilerParams(has_side_effects=True, collective_id=0, vmem_limit_bytes=67043328),
    )(*args)


def local(q_nope, q_rope, cache, w_uk, w_uv, d_out, sel, slot_blocks):
    attn, dqn, dqr, dc = whole(
        q_nope, q_rope, d_out, cache.reshape(16, 4, 16, 576), w_uk, w_uv, sel, slot_blocks
    )
    return (attn, dqn, dqr, dc.astype(F32).reshape(1024, 576))

def solution(mesh):
    return jax.shard_map(
        local,
        mesh=mesh,
        in_specs=(
            P("seq", "grp", None),
            P("seq", "grp", None),
            P("seq", None),
            P("grp", "seq"),
            P("grp", "seq"),
            P("seq", "grp", None),
            P("seq", None),
            P("seq", None),
        ),
        out_specs=(
            P("seq", "grp", None),
            P("seq", "grp", None),
            P("seq", "grp", None),
            P("seq", None),
        ),
        check_vma=False,
    )
```

time: 206 us -> 175 us (0.85)
  Pallas kernels: 197 us -> 166 us
    pallas_call x1, Pallas kernels: 197 us -> 166 us  [whole(): pl.pallas_call(whole_kernel, name='whole', out_shape=(jax.ShapeDtypeStruc...]
where the time goes in v3:
time: 175 us; the launch traced here: 174 us
  Pallas kernels  166 us (95%)
  local copies, waits for them, and re-layouts  6.38 us (4%)
    pallas_call x1, Pallas kernels, whole(): pl.pallas_call(whole_kernel, name='whole', out_shape=(jax.ShapeDtypeStruc...  166 us
    unnamed x11, local copies, waits for them, and re-layouts  6.38 us

profile of v3, /device:TPU:1, one launch (start us, length us, event | category | flops | bytes accessed | tf_op | source)
XLA Modules:
  0.0 174.4 jit_solution(6598579198157138451)
XLA Ops:
  0.6 2.4 %copy.12 = bf16[1024,576]{1,0:T(8,128)(2,1)} copy(bf16[1024,576]{0,1:T(8,128)(2,1)} %param.10) | data formatting | bytes 2359296 | tf_op args[2]
  3.0 165.9 %whole.1 = (bf16[16,32,128]{2,1,0:T(8,128)(2,1)}, bf16[16,32,128]{2,1,0:T(8,128)(2,1)}, bf16[16,32,64]{2,1,0:T(8,128)(2,1)}, bf16[16,4,16,576]{3,2,1,0:T(8,128)(2,1)}) custom-call(bf16[16,32,128]{2,1,0:T(8,128)(2,1)} %qn_in.1, bf16[16,32,64]{2,1,0:T(8,128)(2,1)} %qr_in.1, bf16[16,32,128]{2,1,0:T(8,128)(2,1)} %do_in.1, bf16[16,4,16,576]{3,2,1,0:T(8,128)(2,1)} %bitcast.4, ...), custom_call_target="tpu_custom_call" | custom-call | tf_op jit(solution)/shard_map/whole/pallas_call | solution.py:492
  168.9 1.5 bitcast_convert_fusion
  170.4 0.0 copy-start.2
  170.4 0.0 copy-start.1
  170.5 0.0 copy-start
  170.5 2.0 %copy.13 = f32[1024,576]{0,1:T(8,128)} copy(f32[1024,576]{1,0:T(8,128)S(1)} %bitcast_convert_fusion) | data formatting | bytes 4718592
  172.5 0.0 copy-done.2
  172.5 0.7 copy.17
  173.1 0.0 copy-done.1
  173.1 0.7 copy.18
  173.8 0.0 copy-done
  173.8 0.7 copy.19
Async XLA Ops:
  170.4 2.0 %copy-start.2 = (bf16[16,32,128]{2,1,0:T(8,128)(2,1)S(1)}, bf16[16,32,128]{2,1,0:T(8,128)(2,1)}, u32[]{:S(2)}) copy-start(bf16[16,32,128]{2,1,0:T(8,128)(2,1)} %get-tuple-element.20) | copy-start | bytes 393220
  170.4 2.7 %copy-start.1 = (bf16[16,32,128]{2,1,0:T(8,128)(2,1)S(1)}, bf16[16,32,128]{2,1,0:T(8,128)(2,1)}, u32[]{:S(2)}) copy-start(bf16[16,32,128]{2,1,0:T(8,128)(2,1)} %get-tuple-element.21) | copy-start | bytes 393220
  170.5 3.3 %copy-start = (bf16[16,32,64]{2,1,0:T(8,128)(2,1)S(1)}, bf16[16,32,64]{2,1,0:T(8,128)(2,1)}, u32[]{:S(2)}) copy-start(bf16[16,32,64]{2,1,0:T(8,128)(2,1)} %get-tuple-element.22) | copy-start | bytes 196612

commit v4 on v3

--- a/solution.py
+++ b/solution.py
@@ -48,7 +48,7 @@
 def whole_kernel(qn_in, qr_in, do_in, cache, wk_in, wv_in, sel, slot,
                  attn, dqn, dqr, out,
                  wsh, wall, table, m_ref, send, keys,
-                 qn, do, qf, dol, bias, e_ref, dp_ref, mj_ref, dk,
+                 qn, do, qf, dol, bias, e_ref, dp_ref, mj_ref, part, dk,
                  dqt, ot, ol, dql, at_t, fl, fr, nl, nr, tol, tor, got,
                  sent, zr, yr, yq, sr, ixr, ar, xr, xq, fq, nq, br, gr_, gq, loc):
     si, g, z, y, c = place()
@@ -64,6 +64,7 @@
 
     for i, w_in in ((0, wk_in), (32, wv_in)):
         wsh[i:i + 32] = w_in[...].astype(F32).reshape(32, 8, 128).astype(BF)
+    got[...] = jnp.transpose(cache[...]).reshape(64, 16, 576)
     pl.semaphore_wait(barrier, 65)
 
     def go(src, dst, kind, rsem, seq, grp):
@@ -133,8 +134,10 @@
     qn[...] = jnp.swapaxes(qn_in[...].astype(F32), 0, 1).astype(BF)
     ol[...] = jnp.dot(qn[...].reshape(512, 128), rep, preferred_element_type=F32).astype(BF)
     z_step(0, 1)
+    y_near(0, 0)
     y_send(0, 1)
     y_send(0, 7)
+    z_step(1, 1)
     mine.wait()
     here(table.at[pl.ds(0, 63)], ixr.at[0])
 
@@ -152,7 +155,7 @@
         return carry
 
     lax.fori_loop(0, 8, build, 0)
-    cq = cache[:, g].reshape(256, 576)
+    cq = jnp.concatenate([got[4 * b + g] for b in range(16)], axis=0)
 
     def pick(i, carry):
         rows = pl.ds(8 * i, 8)
@@ -171,23 +174,114 @@
                     to = sid(z + i, y + dy, lax.rem(c + dc, 2))
                     go(send.at[to], keys.at[si, g], 2, ar.at[i], to, g)
 
+    def x_part(i, who, d=None):
+        base = 8 * lax.rem(z + ZN - i, ZN)
+        if d is None:
+            return keys.at[pl.ds(base, 8), who]
+        return keys.at[pl.ds(base + 4 * d, 4), who]
+
+    def x_start(i):
+        ref = x_part(i, g)
+        here(keys.at[pl.ds(0, 7), g] if i == 0 else ref, ar.at[i])
+        go(ref, ref, 3, xr.at[i, 0], si, gr)
+        go(ref, ref, 3, xr.at[i, 1], si, gl)
+
+    def x_fwd(i):
+        for d in range(2):
+            who, to = (gl, gr) if d == 0 else (gr, gl)
+            here(x_part(i, who), xr.at[i, d])
+            go(x_part(i, who, d), x_part(i, who, d), 3, xq.at[i], si, to)
+
+    def x_done(i):
+        here(x_part(i, gf), xq.at[i])
+
+    lb_mask = lax.rem(lax.broadcasted_iota(jnp.int32, (64, 512), 1), 4) == (
+        lax.broadcasted_iota(jnp.int32, (64, 512), 0) // 16
+    )
+
+    def weight(i):
+        return wall[:, i].astype(F32).reshape(512, 128).astype(BF)
+
+    def rows16(h):
+        return pl.ds(pl.multiple_of(16 * h, 16), 16)
+
+    def project_q(h, carry):
+        wide = jnp.where(lb_mask, jnp.concatenate([ol[rows16(h), :].astype(F32)] * 4, axis=0), 0.0).astype(BF)
+        lat = jnp.dot(wide, weight(h), preferred_element_type=F32)
+        qf[rows16(h), 0:512] = jnp.concatenate([lat[16 * b:16 * b + 16] for b in range(4)], axis=1).astype(BF)
+        return carry
+
+    def project_d(h, carry):
+        dol[rows16(h), :] = lax.dot_general(do[h], weight(32 + h), NT, preferred_element_type=F32).astype(BF)
+        return carry
+
+    def chunk_keys(zz):
+        return keys[pl.ds(8 * zz, 8)].reshape(512, 576)
+
+    def score(i, m, l):
+        zz = lax.rem(z + ZN - i, ZN)
+        s = lax.dot_general(chunk_keys(zz), qf[...], NT, preferred_element_type=F32) * SCALE
+        b = bias[pl.ds(pl.multiple_of(8 * zz, 8), 8), :]
+        s = (s.reshape(8, 64, 512) + b[:, None, :]).reshape(512, 512)
+        mn = jnp.maximum(m, jnp.max(s, axis=0, keepdims=True))
+        e = jnp.exp(s - mn)
+        e_ref[zz] = e
+        mj_ref[zz] = mn
+        return mn, l * jnp.exp(m - mn) + jnp.sum(e, axis=0, keepdims=True)
+
+    zero = jnp.zeros((1, 512), F32)
+    state = [zero + NEG, zero]
+
+    def yn(kv, t):
+        y_near(kv, ORDER[t])
+
+    def yf(kv, t):
+        y_far(kv, ORDER[t])
+
+    def ys(kv, t):
+        y_send(kv, ORDER[t])
+
+    def sc(t):
+        x_done(ORDER[t])
+        state[:] = score(ORDER[t], *state)
+
+    def dps(t):
+        zz = lax.rem(z + ZN - ORDER[t], ZN)
+        dp = lax.dot_general(chunk_keys(zz)[:, :512], dol[...], NT, preferred_element_type=F32)
+        dp_ref[zz] = dp
+        part[zz] = jnp.sum(e_ref[zz] * dp, axis=0, keepdims=True)
+
+    def pq(h):
+        lax.fori_loop(h, h + 8, project_q, 0, unroll=2)
+
+    def pd(h):
+        lax.fori_loop(h, h + 8, project_d, 0, unroll=2)
+
+    def xst(t):
+        x_start(ORDER[t])
+
+    def xf(t):
+        x_fwd(ORDER[t])
+
+    z_step(0, 2)
+    yn(0, 1)
+    ys(0, 3)
+    ys(0, 4)
+    yf(0, 0)
+    z_step(1, 2)
     ask(0)
-    z_step(0, 2)
-    y_send(0, 2)
-    y_send(0, 6)
-    z_step(1, 1)
-    y_near(0, 0)
+    yn(0, 2)
+    yf(0, 1)
     z_step(0, 3)
-    y_send(0, 3)
-    y_send(0, 5)
-    z_step(1, 2)
+    ys(0, 5)
+    ys(0, 6)
     ask(1)
     ask(2)
-    y_near(0, 1)
+    yn(0, 3)
+    z_step(1, 3)
     z_step(0, 4)
-    y_send(0, 4)
-    z_step(1, 3)
-    z_step(1, 4)
+    yn(0, 4)
+    ys(0, 7)
     ask(3)
     ask(4)
     ask(5)
@@ -207,180 +301,96 @@
     )
     held = lax.dot_general(chosen.astype(BF), spread.astype(BF), TN, preferred_element_type=F32)
     bias[...] = jnp.where(held > 0.5, 0.0, NEG)
-
-    def x_part(i, who, d=None):
-        base = 8 * lax.rem(z + ZN - i, ZN)
-        if d is None:
-            return keys.at[pl.ds(base, 8), who]
-        return keys.at[pl.ds(base + 4 * d, 4), who]
-
-    def x_start(i):
-        ref = x_part(i, g)
-        here(keys.at[pl.ds(0, 7), g] if i == 0 else ref, ar.at[i])
-        go(ref, ref, 3, xr.at[i, 0], si, gr)
-        go(ref, ref, 3, xr.at[i, 1], si, gl)
-
-    def x_fwd(i):
-        for d in range(2):
-            who, to = (gl, gr) if d == 0 else (gr, gl)
-            here(x_part(i, who), xr.at[i, d])
-            go(x_part(i, who, d), x_part(i, who, d), 3, xq.at[i], si, to)
-
-    def x_done(i):
-        here(x_part(i, gf), xq.at[i])
-
-    lb_mask = lax.rem(lax.broadcasted_iota(jnp.int32, (64, 512), 1), 4) == (
-        lax.broadcasted_iota(jnp.int32, (64, 512), 0) // 16
-    )
-
-    def weight(i):
-        return wall[:, i].astype(F32).reshape(512, 128).astype(BF)
-
-    def rows16(h):
-        return pl.ds(pl.multiple_of(16 * h, 16), 16)
-
-    def project_q(h, carry):
-        wide = jnp.where(lb_mask, jnp.concatenate([ol[rows16(h), :].astype(F32)] * 4, axis=0), 0.0).astype(BF)
-        lat = jnp.dot(wide, weight(h), preferred_element_type=F32)
-        qf[rows16(h), 0:512] = jnp.concatenate([lat[16 * b:16 * b + 16] for b in range(4)], axis=1).astype(BF)
-        return carry
-
-    def project_d(h, carry):
-        dol[rows16(h), :] = lax.dot_general(do[h], weight(32 + h), NT, preferred_element_type=F32).astype(BF)
-        return carry
-
-    def chunk_keys(zz):
-        return keys[pl.ds(8 * zz, 8)].reshape(512, 576)
-
-    def score(i, m, l):
-        zz = lax.rem(z + ZN - i, ZN)
-        s = lax.dot_general(chunk_keys(zz), qf[...], NT, preferred_element_type=F32) * SCALE
-        b = bias[pl.ds(pl.multiple_of(8 * zz, 8), 8), :]
-        s = (s.reshape(8, 64, 512) + b[:, None, :]).reshape(512, 512)
-        mn = jnp.maximum(m, jnp.max(s, axis=0, keepdims=True))
-        e = jnp.exp(s - mn)
-        e_ref[zz] = e
-        mj_ref[zz] = mn
-        return mn, l * jnp.exp(m - mn) + jnp.sum(e, axis=0, keepdims=True)
-
-    zero = jnp.zeros((1, 512), F32)
-    state = [zero + NEG, zero]
-
-    def yn(kv, t):
-        y_near(kv, ORDER[t])
-
-    def yf(kv, t):
-        y_far(kv, ORDER[t])
-
-    def ys1(t):
-        y_send(1, ORDER[t])
-
-    def sc(t):
-        x_done(ORDER[t])
-        state[:] = score(ORDER[t], *state)
-
-    def pq(h):
-        lax.fori_loop(h, h + 8, project_q, 0, unroll=2)
-
-    def pd(h):
-        lax.fori_loop(h, h + 8, project_d, 0, unroll=2)
-
-    def xst(t):
-        x_start(ORDER[t])
-
-    def xf(t):
-        x_fwd(ORDER[t])
-
     xst(0)
-    yf(0, 0)
-    yn(0, 2)
+    yf(0, 2)
+    yn(0, 5)
+    yn(0, 6)
     xf(0)
     xst(1)
-    yf(0, 1)
-    yn(0, 3)
+    yf(0, 3)
+    yf(0, 4)
     xst(2)
+    z_step(1, 4)
+    yn(0, 7)
+    ys(1, 0)
+    ys(1, 1)
+    ys(1, 2)
+    ys(1, 3)
+    ys(1, 4)
+    ys(1, 5)
+    ys(1, 6)
+    ys(1, 7)
     xf(1)
-    yn(0, 4)
-    yf(0, 2)
     xf(2)
-    yn(0, 5)
-    yf(0, 3)
-    yn(0, 6)
-    yf(0, 4)
     xst(3)
-    yn(0, 7)
+    xst(4)
     yf(0, 5)
-    ys1(0)
-    ys1(1)
-    ys1(2)
-    ys1(3)
-    ys1(4)
-    ys1(5)
-    ys1(6)
-    ys1(7)
-    xst(4)
-    xf(3)
     yf(0, 6)
     yf(0, 7)
-    xf(4)
+    xf(3)
     sib_wait(0)
     pq(0)
+    yn(1, 0)
     pq(8)
-    yn(1, 0)
     pq(16)
+    yn(1, 1)
+    xf(4)
     pq(24)
+    yn(1, 2)
     sc(0)
     sc(1)
-    yn(1, 1)
-    yf(1, 0)
+    yn(1, 3)
     sc(2)
     xst(5)
-    yn(1, 2)
+    sc(3)
+    yn(1, 4)
+    xst(6)
+    sc(4)
+    yn(1, 5)
+    yn(1, 6)
+    yn(1, 7)
+    yf(1, 0)
     yf(1, 1)
-    sc(3)
-    xst(6)
+    yf(1, 2)
+    yf(1, 3)
     xf(5)
-    yn(1, 3)
-    yf(1, 2)
-    sc(4)
+    yf(1, 4)
+    xst(7)
+    yf(1, 5)
     xf(6)
-    yn(1, 4)
-    yf(1, 3)
-    xst(7)
-    yn(1, 5)
-    yf(1, 4)
-    sc(5)
-    yn(1, 6)
-    yf(1, 5)
-    sc(6)
-    yn(1, 7)
-    xf(7)
     yf(1, 6)
     yf(1, 7)
+    sc(5)
     sib_wait(1)
     pd(0)
     pd(8)
     pd(16)
     pd(24)
+    xf(7)
+    dps(0)
+    dps(1)
+    dps(2)
+    dps(3)
+    dps(4)
+    dps(5)
+    sc(6)
+    dps(6)
     sc(7)
+    dps(7)
     m, l = state
     inv = 1.0 / l
 
-    def back(j, d):
-        p = e_ref[j] * (jnp.exp(mj_ref[j] - m) * inv)
-        dp = lax.dot_general(keys[pl.ds(8 * j, 8)].reshape(512, 576)[:, :512], dol[...], NT, preferred_element_type=F32)
-        e_ref[j] = p
-        dp_ref[j] = dp
-        return d + jnp.sum(p * dp, axis=0, keepdims=True)
-
-    delta = lax.fori_loop(0, 8, back, zero)
+    delta = zero
+    for i in range(8):
+        delta += jnp.exp(mj_ref[i] - m) * part[i]
+    delta = delta * inv
     dqt[...] = jnp.zeros_like(dqt)
     ot[...] = jnp.zeros_like(ot)
 
     def grads(i):
         zz = lax.rem(z + i, ZN)
         kj = chunk_keys(zz)
-        p = e_ref[zz]
+        p = e_ref[zz] * (jnp.exp(mj_ref[zz] - m) * inv)
         pb = p.astype(BF)
         ds = (p * (dp_ref[zz] - delta) * SCALE).astype(BF)
         gk = jnp.dot(ds, qf[...], preferred_element_type=F32)
@@ -504,7 +514,7 @@
             v((64, 8, 128), BF), v((64, 64, 8, 128), BF), v((64, 1, 64), jnp.int32), v((64, 16, 256), BF), quarter,
             v((64, 4, 16, 576), BF),
             v((32, 16, 128), BF), v((32, 16, 128), BF), v((512, 576), BF), v((512, 512), BF), v((64, 512), F32),
-            v((8, 512, 512), F32), v((8, 512, 512), F32), v((8, 1, 512), F32), v((64, 4, 16, 576), BF),
+            v((8, 512, 512), F32), v((8, 512, 512), F32), v((8, 1, 512), F32), v((8, 1, 512), F32), v((64, 4, 16, 576), BF),
             v((576, 512), F32), v((512, 512), F32), v((512, 512), BF), v((512, 512), BF),
             quarter, half, half, quarter, quarter, half, half, quarter,
             dma((7,)), dma((2, 2, 4)), dma((2, 8, 2)), dma((2, 8)), dma((2,)), dma((1,)), dma((8,)),
@@ -516,7 +526,7 @@
 
 def local(q_nope, q_rope, cache, w_uk, w_uv, d_out, sel, slot_blocks):
     attn, dqn, dqr, dc = whole(
-        q_nope, q_rope, d_out, cache.reshape(16, 4, 16, 576), w_uk, w_uv, sel, slot_blocks
+        q_nope, q_rope, d_out, cache.T, w_uk, w_uv, sel, slot_blocks
     )
     return (attn, dqn, dqr, dc.astype(F32).reshape(1024, 576))
 

time: 175 us -> 162 us (0.926)
  Pallas kernels: 166 us -> 155 us
  local copies, waits for them, and re-layouts: 6.38 us -> 3.97 us
    pallas_call x1, Pallas kernels: 166 us -> 155 us  [whole(): pl.pallas_call(whole_kernel, name='whole', out_shape=(jax.ShapeDtypeStruc...]
    unnamed x11 -> x10, local copies, waits for them, and re-layouts: 6.38 us -> 3.97 us
where the time goes in v4:
time: 162 us
  Pallas kernels  155 us (96%)
  local copies, waits for them, and re-layouts  3.97 us (2%)
    pallas_call x1, Pallas kernels, whole(): pl.pallas_call(whole_kernel, name='whole', out_shape=(jax.ShapeDtypeStruc...  155 us
    unnamed x10, local copies, waits for them, and re-layouts  3.97 us

profile of v4, /device:TPU:1, one launch (start us, length us, event | category | flops | bytes accessed | tf_op | source)
XLA Modules:
  0.0 161.6 jit_solution(1991687269636414909)
XLA Ops:
  0.6 155.5 %whole.1 = (bf16[16,32,128]{2,1,0:T(8,128)(2,1)}, bf16[16,32,128]{2,1,0:T(8,128)(2,1)}, bf16[16,32,64]{2,1,0:T(8,128)(2,1)}, bf16[16,4,16,576]{3,2,1,0:T(8,128)(2,1)}) custom-call(bf16[16,32,128]{2,1,0:T(8,128)(2,1)} %qn_in.1, bf16[16,32,64]{2,1,0:T(8,128)(2,1)} %qr_in.1, bf16[16,32,128]{2,1,0:T(8,128)(2,1)} %do_in.1, bf16[576,1024]{1,0:T(8,128)(2,1)} %bitcast.4, ...), custom_call_target="tpu_custom_call" | custom-call | tf_op jit(solution)/shard_map/whole/pallas_call | solution.py:502
  156.1 1.5 bitcast_convert_fusion
  157.6 0.0 copy-start.2
  157.6 0.0 copy-start.1
  157.6 0.0 copy-start
  157.6 2.0 %copy.12 = f32[1024,576]{0,1:T(8,128)} copy(f32[1024,576]{1,0:T(8,128)S(1)} %bitcast_convert_fusion) | data formatting | bytes 4718592
  159.6 0.0 copy-done.2
  159.6 0.7 copy.16
  160.3 0.0 copy-done.1
  160.3 0.7 copy.17
  160.9 0.0 copy-done
  160.9 0.7 copy.18
Async XLA Ops:
  157.6 2.0 %copy-start.2 = (bf16[16,32,128]{2,1,0:T(8,128)(2,1)S(1)}, bf16[16,32,128]{2,1,0:T(8,128)(2,1)}, u32[]{:S(2)}) copy-start(bf16[16,32,128]{2,1,0:T(8,128)(2,1)} %get-tuple-element.20) | copy-start | bytes 393220
  157.6 2.7 %copy-start.1 = (bf16[16,32,128]{2,1,0:T(8,128)(2,1)S(1)}, bf16[16,32,128]{2,1,0:T(8,128)(2,1)}, u32[]{:S(2)}) copy-start(bf16[16,32,128]{2,1,0:T(8,128)(2,1)} %get-tuple-element.21) | copy-start | bytes 393220
  157.6 3.3 %copy-start = (bf16[16,32,64]{2,1,0:T(8,128)(2,1)S(1)}, bf16[16,32,64]{2,1,0:T(8,128)(2,1)}, u32[]{:S(2)}) copy-start(bf16[16,32,64]{2,1,0:T(8,128)(2,1)} %get-tuple-element.22) | copy-start | bytes 196612

commit v5 on v4

--- a/solution.py
+++ b/solution.py
@@ -46,10 +46,11 @@
 
 
 def whole_kernel(qn_in, qr_in, do_in, cache, wk_in, wv_in, sel, slot,
-                 attn, dqn, dqr, out,
+                 attn, dqn, dqr, flip0, flip1,
                  wsh, wall, table, m_ref, send, keys,
-                 qn, do, qf, dol, bias, e_ref, dp_ref, mj_ref, part, dk,
-                 dqt, ot, ol, dql, at_t, fl, fr, nl, nr, tol, tor, got,
+                 qn, do, qf, dol, bias, e_ref, dp_ref, mj_ref, part,
+                 dqt, ot, ol, dql, cs, dk0, dk1, dk2, fl0, fl1, fl2, fr0, fr1, fr2,
+                 nl0, nl1, nl2, nr0, nr1, nr2, tl0, tl1, tl2, tr0, tr1, tr2, bs0, bs1, got0, got1, out0, out1,
                  sent, zr, yr, yq, sr, ixr, ar, xr, xq, fq, nq, br, gr_, gq, loc):
     si, g, z, y, c = place()
     zp, zm = sid(z + 1, y, c), sid(z + 7, y, c)
@@ -64,7 +65,7 @@
 
     for i, w_in in ((0, wk_in), (32, wv_in)):
         wsh[i:i + 32] = w_in[...].astype(F32).reshape(32, 8, 128).astype(BF)
-    got[...] = jnp.transpose(cache[...]).reshape(64, 16, 576)
+    cs[...] = jnp.transpose(cache[...]).reshape(64, 16, 576)
     pl.semaphore_wait(barrier, 65)
 
     def go(src, dst, kind, rsem, seq, grp):
@@ -155,7 +156,7 @@
         return carry
 
     lax.fori_loop(0, 8, build, 0)
-    cq = jnp.concatenate([got[4 * b + g] for b in range(16)], axis=0)
+    cq = jnp.concatenate([cs[4 * b + g] for b in range(16)], axis=0)
 
     def pick(i, carry):
         rows = pl.ds(8 * i, 8)
@@ -253,9 +254,6 @@
 
     def pq(h):
         lax.fori_loop(h, h + 8, project_q, 0, unroll=2)
-
-    def pd(h):
-        lax.fori_loop(h, h + 8, project_d, 0, unroll=2)
 
     def xst(t):
         x_start(ORDER[t])
@@ -362,10 +360,7 @@
     yf(1, 7)
     sc(5)
     sib_wait(1)
-    pd(0)
-    pd(8)
-    pd(16)
-    pd(24)
+    lax.fori_loop(0, 32, project_d, 0, unroll=4)
     xf(7)
     dps(0)
     dps(1)
@@ -395,63 +390,130 @@
         ds = (p * (dp_ref[zz] - delta) * SCALE).astype(BF)
         gk = jnp.dot(ds, qf[...], preferred_element_type=F32)
         gv = jnp.dot(pb, dol[...], preferred_element_type=F32)
-        gk = jnp.concatenate([gk[:, :512] + gv, gk[:, 512:]], axis=1)
-        dk[pl.ds(8 * zz, 8)] = gk.astype(BF).reshape(8, 4, 16, 576)
+        gr8 = pl.ds(8 * zz, 8)
+        dk0[gr8] = (gk[:, :256] + gv[:, :256]).astype(BF).reshape(8, 4, 16, 256)
+        dk1[gr8] = (gk[:, 256:512] + gv[:, 256:]).astype(BF).reshape(8, 4, 16, 256)
+        pair = gk[:, 512:].reshape(4, 2, 64, 64)
+        pair = jnp.concatenate([pair[:, 0], pair[:, 1]], axis=2)
+        dk2[pl.ds(4 * zz, 4)] = pair.astype(BF).reshape(4, 4, 16, 128)
         dqt[...] += lax.dot_general(kj, ds, TN, preferred_element_type=F32)
         ot[...] += lax.dot_general(kj[:, :512], pb, TN, preferred_element_type=F32)
 
-    def lo(i):
-        return pl.ds(8 * lax.rem(z + i, ZN), 4)
-
-    def hi(i):
-        return pl.ds(8 * lax.rem(z + i, ZN) + 4, 4)
-
-    def leave(i):
-        go(dk.at[lo(i), gf], fl.at[i], 4, fq.at[i, 0], si, gr)
-        go(dk.at[hi(i), gf], fr.at[i], 4, fq.at[i, 1], si, gl)
-        go(dk.at[hi(i), gr], nl.at[hi(i)], 4, nq.at[i], si, gr)
-        go(dk.at[lo(i), gl], nr.at[lo(i)], 4, nq.at[i], si, gl)
-
-    def combine(i):
-        here(fl.at[i], fq.at[i, 0])
-        tor[i] = (dk[lo(i), gr].astype(F32) + fl[i].astype(F32)).astype(BF)
-        here(fr.at[i], fq.at[i, 1])
-        tol[i] = (dk[hi(i), gl].astype(F32) + fr[i].astype(F32)).astype(BF)
-        go(tor.at[i], nl.at[lo(i)], 4, nq.at[i], si, gr)
-        go(tol.at[i], nr.at[hi(i)], 4, nq.at[i], si, gl)
-
-    def owner(i):
-        here(dk.at[pl.ds(0, 4)], nq.at[i])
+    dks, fls, frs = (dk0, dk1, dk2), (fl0, fl1, fl2), (fr0, fr1, fr2)
+    nls, nrs, tls, trs = (nl0, nl1, nl2), (nr0, nr1, nr2), (tl0, tl1, tl2), (tr0, tr1, tr2)
+    parts = ((1, 2), (0,))
+    backs, gots, outs = (bs1, bs0), (got1, got0), (out1, out0)
+
+    def span(i, k, h):
+        n = 2 if k == 2 else 4
+        return pl.ds(2 * n * lax.rem(z + i, ZN) + n * h, n)
+
+    def leave(p, t):
+        i = RORDER[t]
+        for k in parts[p]:
+            lo, hi = span(i, k, 0), span(i, k, 1)
+            go(dks[k].at[lo, gf], fls[k].at[i], 4 + k, fq.at[k, i, 0], si, gr)
+            go(dks[k].at[hi, gf], frs[k].at[i], 4 + k, fq.at[k, i, 1], si, gl)
+            go(dks[k].at[hi, gr], nls[k].at[hi], 4 + k, nq.at[k, i], si, gr)
+            go(dks[k].at[lo, gl], nrs[k].at[lo], 4 + k, nq.at[k, i], si, gl)
+
+    def combine(p, t):
+        i = RORDER[t]
+        for k in parts[p]:
+            lo, hi = span(i, k, 0), span(i, k, 1)
+            here(fls[k].at[i], fq.at[k, i, 0])
+            trs[k][i] = (dks[k][lo, gr].astype(F32) + fls[k][i].astype(F32)).astype(BF)
+            here(frs[k].at[i], fq.at[k, i, 1])
+            tls[k][i] = (dks[k][hi, gl].astype(F32) + frs[k][i].astype(F32)).astype(BF)
+            go(trs[k].at[i], nls[k].at[lo], 4 + k, nq.at[k, i], si, gr)
+            go(tls[k].at[i], nrs[k].at[hi], 4 + k, nq.at[k, i], si, gl)
+
+    def total_of(i, k):
+        n = 4 if k == 2 else 8
+        here(dks[k].at[pl.ds(0, n // 2)], nq.at[k, i])
+        al = pl.ds(n * lax.rem(z + i, ZN), n)
+        return dks[k][al, g].astype(F32) + nls[k][al].astype(F32) + nrs[k][al].astype(F32)
+
+    def owner(p, t):
+        i = RORDER[t]
         al = pl.ds(8 * lax.rem(z + i, ZN), 8)
-        back_send[al] = (dk[al, g].astype(F32) + nl[al].astype(F32) + nr[al].astype(F32)).astype(BF)
+        if p == 1:
+            bs0[al] = total_of(i, 0).astype(BF)
+        else:
+            pair = total_of(i, 2)
+            pair = jnp.stack([pair[:, :, :64], pair[:, :, 64:]], axis=1).reshape(8, 16, 64)
+            bs1[al] = jnp.concatenate([total_of(i, 1), pair], axis=2).astype(BF)
         for dy in range(YN):
             for dc in range(2):
                 if (i, dy, dc) != (0, 0, 0):
                     to = sid(z + i, y + dy, lax.rem(c + dc, 2))
-                    go(back_send.at[to], got.at[si], 5, br.at[0], to, g)
-
-    back_send = at_t
+                    go(backs[p].at[to], gots[p].at[si], 7 + p, br.at[p], to, g)
+
+    def share(p):
+        gots[p][si] = backs[p][si]
+        here(gots[p].at[pl.ds(0, 63)], br.at[p])
+        w = 320 if p == 0 else 256
+        total = lax.dot_general(
+            m_ref[...].reshape(1024, 256), gots[p][...].reshape(1024, w), TN, preferred_element_type=F32
+        )
+        outs[p][:, g] = total.astype(BF).reshape(16, 16, w)
+        for h in range(2):
+            for d in range(2):
+                ref = outs[p].at[pl.ds(8 * (h ^ d), 8), g]
+                go(ref, ref, 9 + p, gr_.at[p, d, h], si, gr if d == 0 else gl)
+
+    def pass_on(p):
+        for d in range(2):
+            who, to = (gl, gr) if d == 0 else (gr, gl)
+            h = outs[p].at[pl.ds(8 * d, 8), who]
+            here(h, gr_.at[p, d, 0])
+            go(h, h, 9 + p, gq.at[p], si, to)
+
+    def near_rest(p):
+        for d in range(2):
+            here(outs[p].at[pl.ds(8 - 8 * d, 8), gl if d == 0 else gr], gr_.at[p, d, 1])
+
     for t in range(8):
         grads(RORDER[t])
-        leave(RORDER[t])
-        if t >= 2:
-            combine(RORDER[t - 2])
-        if t >= 4:
-            owner(RORDER[t - 4])
-    combine(RORDER[6])
-    owner(RORDER[4])
+        leave(0, t)
+        if t >= 3:
+            combine(0, t - 3)
+        if t >= 5:
+            owner(0, t - 5)
+    leave(1, 0)
+    combine(0, 5)
+    owner(0, 3)
+    leave(1, 1)
+    combine(0, 6)
+    owner(0, 4)
+    leave(1, 2)
+    combine(0, 7)
+    owner(0, 5)
+    combine(1, 0)
+    leave(1, 3)
+    owner(0, 6)
+    combine(1, 1)
+    owner(0, 7)
+    leave(1, 4)
+    owner(1, 0)
+    combine(1, 2)
+    leave(1, 5)
     gone(wall.at[pl.ds(0, 63)], 0)
     gone(table.at[pl.ds(0, 63)], 1)
     gone(send.at[pl.ds(0, 63)], 2)
     gone(keys.at[pl.ds(0, 48)], 3)
+    owner(1, 1)
+    combine(1, 3)
+    leave(1, 6)
+    owner(1, 2)
+    share(0)
+    combine(1, 4)
+    leave(1, 7)
+    owner(1, 3)
+    combine(1, 5)
     ol[...] = jnp.transpose(ot[...]).astype(BF)
-    combine(RORDER[7])
-    owner(RORDER[5])
     dql[...] = jnp.transpose(dqt[0:512, :]).astype(BF)
-    owner(RORDER[6])
     dqr[...] = jnp.swapaxes(jnp.transpose(dqt[512:576, :]).reshape(32, 16, 64), 0, 1).astype(BF)
-    owner(RORDER[7])
-    got[si] = back_send[si]
 
     def finish(h, carry):
         qn[h] = jnp.dot(ol[rows16(h), :], weight(32 + h), preferred_element_type=F32).astype(BF)
@@ -463,14 +525,22 @@
         return carry
 
     lax.fori_loop(0, 32, finish, 0, unroll=2)
-    here(got.at[pl.ds(0, 63)], br.at[0])
-    total = lax.dot_general(m_ref[...].reshape(1024, 256), got[...].reshape(1024, 576), TN, preferred_element_type=F32)
-    out[:, g] = total.astype(BF).reshape(16, 16, 576)
-    ref = out.at[:, g]
-    go(ref, ref, 6, gr_.at[0], si, gr)
-    go(ref, ref, 6, gr_.at[1], si, gl)
-    gone(dk.at[pl.ds(0, 48)], 4)
-    gone(back_send.at[pl.ds(0, 63)], 5)
+    owner(1, 4)
+    pass_on(0)
+    combine(1, 6)
+    owner(1, 5)
+    combine(1, 7)
+    owner(1, 6)
+    owner(1, 7)
+
+    share(1)
+    near_rest(0)
+    here(outs[0].at[:, gf], gq.at[0])
+    flip1[...] = jnp.transpose(out1[...].reshape(1024, 320))
+    for k, n in ((0, 48), (1, 48), (2, 24)):
+        gone(dks[k].at[pl.ds(0, n)], 4 + k)
+    for p in range(2):
+        gone(backs[p].at[pl.ds(0, 63)], 7 + p)
     attn[...] = jnp.swapaxes(qn[...].astype(F32), 0, 1).astype(BF)
     gv0 = ot[...]
     g0 = gv0.astype(BF)
@@ -481,13 +551,12 @@
     acc += lax.dot_general(g1, rep, NT, preferred_element_type=F32)
     acc += lax.dot_general(g2, rep, NT, preferred_element_type=F32)
     dqn[...] = jnp.swapaxes(acc.reshape(32, 16, 128), 0, 1).astype(BF)
-    for d in range(2):
-        who, to = (gl, gr) if d == 0 else (gr, gl)
-        here(out.at[:, who], gr_.at[d])
-        h = out.at[pl.ds(8 * d, 8), who]
-        go(h, h, 6, gq.at[0], si, to)
-    here(out.at[:, gf], gq.at[0])
-    gone(out.at[pl.ds(0, 12)], 6)
+    pass_on(1)
+    near_rest(1)
+    here(outs[1].at[:, gf], gq.at[1])
+    flip0[...] = jnp.transpose(out0[...].reshape(1024, 256))
+    for p in range(2):
+        gone(outs[p].at[pl.ds(0, 12)], 9 + p)
 
 
 def vm():
@@ -497,8 +566,9 @@
 def whole(*args):
     dma = pltpu.SemaphoreType.DMA
     v = pltpu.VMEM
-    half = v((8, 4, 16, 576), BF)
     quarter = v((64, 16, 576), BF)
+    two = (v((8, 4, 16, 256), BF), v((8, 4, 16, 256), BF), v((8, 2, 16, 128), BF))
+    all3 = (v((64, 16, 256), BF), v((64, 16, 256), BF), v((32, 16, 128), BF))
     return pl.pallas_call(
         whole_kernel,
         name="whole",
@@ -506,29 +576,34 @@
             jax.ShapeDtypeStruct((16, 32, 128), BF),
             jax.ShapeDtypeStruct((16, 32, 128), BF),
             jax.ShapeDtypeStruct((16, 32, 64), BF),
-            jax.ShapeDtypeStruct((16, 4, 16, 576), BF),
+            jax.ShapeDtypeStruct((256, 1024), BF),
+            jax.ShapeDtypeStruct((320, 1024), BF),
         ),
         in_specs=[vm()] * 8,
-        out_specs=(vm(),) * 4,
+        out_specs=(vm(),) * 5,
         scratch_shapes=[
             v((64, 8, 128), BF), v((64, 64, 8, 128), BF), v((64, 1, 64), jnp.int32), v((64, 16, 256), BF), quarter,
             v((64, 4, 16, 576), BF),
             v((32, 16, 128), BF), v((32, 16, 128), BF), v((512, 576), BF), v((512, 512), BF), v((64, 512), F32),
-            v((8, 512, 512), F32), v((8, 512, 512), F32), v((8, 1, 512), F32), v((8, 1, 512), F32), v((64, 4, 16, 576), BF),
-            v((576, 512), F32), v((512, 512), F32), v((512, 512), BF), v((512, 512), BF),
-            quarter, half, half, quarter, quarter, half, half, quarter,
-            dma((7,)), dma((2, 2, 4)), dma((2, 8, 2)), dma((2, 8)), dma((2,)), dma((1,)), dma((8,)),
-            dma((8, 2)), dma((8,)), dma((8, 2)), dma((8,)), dma((1,)), dma((2,)), dma((1,)), dma((2,)),
+            v((8, 512, 512), F32), v((8, 512, 512), F32), v((8, 1, 512), F32), v((8, 1, 512), F32),
+            v((576, 512), F32), v((512, 512), F32), v((512, 512), BF), v((512, 512), BF), quarter,
+            v((64, 4, 16, 256), BF), v((64, 4, 16, 256), BF), v((32, 4, 16, 128), BF),
+            *two, *two, *all3, *all3, *two, *two,
+            v((64, 16, 256), BF), v((64, 16, 320), BF), v((64, 16, 256), BF), v((64, 16, 320), BF),
+            v((16, 4, 16, 256), BF), v((16, 4, 16, 320), BF),
+            dma((11,)), dma((2, 2, 4)), dma((2, 8, 2)), dma((2, 8)), dma((2,)), dma((1,)), dma((8,)),
+            dma((8, 2)), dma((8,)), dma((3, 8, 2)), dma((3, 8)), dma((2,)), dma((2, 2, 2)), dma((2,)), dma((2,)),
         ],
         compiler_params=pltpu.CompilerParams(has_side_effects=True, collective_id=0, vmem_limit_bytes=67043328),
     )(*args)
 
 
 def local(q_nope, q_rope, cache, w_uk, w_uv, d_out, sel, slot_blocks):
-    attn, dqn, dqr, dc = whole(
+    attn, dqn, dqr, dc0, dc1 = whole(
         q_nope, q_rope, d_out, cache.T, w_uk, w_uv, sel, slot_blocks
     )
-    return (attn, dqn, dqr, dc.astype(F32).reshape(1024, 576))
+    dc = jnp.concatenate([dc0, dc1], axis=0).astype(F32)
+    return (attn, dqn, dqr, dc.T)
 
 def solution(mesh):
     return jax.shard_map(

time: 162 us -> 157 us (0.969)
  Pallas kernels: 155 us -> 151 us
  local copies, waits for them, and re-layouts: 3.97 us -> 1.98 us
    pallas_call x1, Pallas kernels: 155 us -> 151 us  [whole(): pl.pallas_call(whole_kernel, name='whole', out_shape=(jax.ShapeDtypeStruc...]
    transpose x0 -> x1, other arithmetic: none -> 2.98 us  [local(): return (attn, dqn, dqr, dc.T)]
    unnamed x10 -> x9, local copies, waits for them, and re-layouts: 3.97 us -> 1.98 us
where the time goes in v5:
time: 157 us
  Pallas kernels  151 us (96%)
  other arithmetic  2.98 us (2%)
  local copies, waits for them, and re-layouts  1.98 us (1%)
    pallas_call x1, Pallas kernels, whole(): pl.pallas_call(whole_kernel, name='whole', out_shape=(jax.ShapeDtypeStruc...  151 us

profile of v5, /device:TPU:1, one launch (start us, length us, event | category | flops | bytes accessed | tf_op | source)
XLA Modules:
  0.0 157.0 jit_solution(4077515987028477572)
XLA Ops:
  0.6 151.3 %whole.1 = (bf16[16,32,128]{2,1,0:T(8,128)(2,1)}, bf16[16,32,128]{2,1,0:T(8,128)(2,1)}, bf16[16,32,64]{2,1,0:T(8,128)(2,1)}, bf16[256,1024]{1,0:T(8,128)(2,1)}, bf16[320,1024]{1,0:T(8,128)(2,1)}) custom-call(bf16[16,32,128]{2,1,0:T(8,128)(2,1)} %qn_in.1, bf16[16,32,64]{2,1,0:T(8,128)(2,1)} %qr_in.1, bf16[16,32,128]{2,1,0:T(8,128)(2,1)} %do_in.1, ...), custom_call_target="tpu_custom_call" | custom-call | tf_op jit(solution)/shard_map/whole/pallas_call | solution.py:572
  152.0 0.0 copy-start.2
  152.0 0.0 copy-start.1
  152.0 0.0 copy-start
  152.0 3.0 %convert_bitcast_fusion = f32[1024,576]{0,1:T(8,128)} fusion(bf16[320,1024]{1,0:T(8,128)(2,1)} %get-tuple-element.13, bf16[256,1024]{1,0:T(8,128)(2,1)} %get-tuple-element.12), kind=kLoop, calls=%fused_computation | loop fusion | flops 2359296 | bytes 3538944 | tf_op jit(solution)/shard_map/transpose | solution.py:606
  155.0 0.0 copy-done.2
  155.0 0.7 copy.15
  155.6 0.0 copy-done.1
  155.6 0.7 copy.16
  156.3 0.0 copy-done
  156.3 0.7 copy.17
Async XLA Ops:
  152.0 3.0 %copy-start.2 = (bf16[16,32,128]{2,1,0:T(8,128)(2,1)S(1)}, bf16[16,32,128]{2,1,0:T(8,128)(2,1)}, u32[]{:S(2)}) copy-start(bf16[16,32,128]{2,1,0:T(8,128)(2,1)} %get-tuple-element.18) | copy-start | bytes 393220
  152.0 3.7 %copy-start.1 = (bf16[16,32,128]{2,1,0:T(8,128)(2,1)S(1)}, bf16[16,32,128]{2,1,0:T(8,128)(2,1)}, u32[]{:S(2)}) copy-start(bf16[16,32,128]{2,1,0:T(8,128)(2,1)} %get-tuple-element.19) | copy-start | bytes 393220
  152.0 4.3 %copy-start = (bf16[16,32,64]{2,1,0:T(8,128)(2,1)S(1)}, bf16[16,32,64]{2,1,0:T(8,128)(2,1)}, u32[]{:S(2)}) copy-start(bf16[16,32,64]{2,1,0:T(8,128)(2,1)} %get-tuple-element.20) | copy-start | bytes 196612
